TPU v7x, 32 devices: a whole 2x2x4 slice. The times are simulated.
32 devices in a mesh: lat: 4 (over z), lon: 8 (over y, x, core).
Axes of the slice: x: 2, y: 2, z: 4, core: 2. Of those that a mesh axis runs over, the one named last changes fastest.
Arguments:
- covariance: float32 [4, 4, 128, 128], P('lat', None, 'lon'), may hold values from -6 to 6
- winds: float32 [2, 3, 4, 128], P(None, None, None, 'lon'), may hold values from -0.35 to 0.35
- diffusivity: float32 [4, 128], P(None, 'lon'), may hold values from 0.01 to 0.07
- cutoff: int32 [4], replicated, may hold values from 0 to 1, as said below
Outputs:
- forecast: float32 [4, 4, 128, 128], P('lat', None, 'lon')
Inputs may be any that keep to these rules, and one draw needn't show every extreme that they name: Some latitude has cutoff 1 and some other has 0.
All inputs are finite; a program needn't handle non-finite values.
Results may differ from a plain program's by a relative error of at most 0.00002.
Values sent between devices are 32-bit elements; how exact they have to be, the bound alone decides.
No kernel may reach another device: no remote copies, remote signals or barrier semaphores. Data moves between devices by JAX's collectives and lax.ppermute only.
A program may use at most 192 MiB of HBM per device.

v0:
```python
import jax
import jax.numpy as jnp
from jax import lax
from jax.sharding import PartitionSpec as P

STEPS = 3


def extended_2(block, sides, width):
    for axis, dim in sides:
        count = lax.axis_size(axis)
        forward = [(i, i + 1) for i in range(count - 1)]
        forward.append((count - 1, 0))
        backward = [(target, source) for source, target in forward]
        low = lax.ppermute(
            lax.slice_in_dim(block, block.shape[dim] - width, None, axis=dim), axis, forward
        )
        high = lax.ppermute(lax.slice_in_dim(block, 0, width, axis=dim), axis, backward)
        block = jnp.concatenate([low, block, high], axis=dim)
    return block


def from_behind(shard, axis, by):
    length = lax.axis_size(axis)
    pairs = [(i, i + by) for i in range(length) if 0 <= i + by < length]
    return lax.ppermute(shard, axis, pairs)


def advance(extended, east_wind, north_wind, spread):
    center = extended[:, :, 1:-1]
    western = extended[:, :, :-2]
    eastern = extended[:, :, 2:]
    zeros_row = jnp.zeros_like(center[:, :1])
    southern = jnp.concatenate([zeros_row, center[:, :-1]], axis=1)
    northern = jnp.concatenate([center[:, 1:], zeros_row], axis=1)
    east_wind = east_wind[None, :, :, None]
    north_wind = north_wind[None, :, :, None]
    spread = spread[None, :, :, None]
    transport = (
        jnp.maximum(east_wind, 0.0) * (center - western)
        + jnp.minimum(east_wind, 0.0) * (eastern - center)
        + jnp.maximum(north_wind, 0.0) * (center - southern)
        + jnp.minimum(north_wind, 0.0) * (northern - center)
    )
    return center - transport + spread * (eastern + western + northern + southern - 4.0 * center)


def propagate(state_field, widened):
    lon_local = state_field.shape[2]
    extended = extended_2(state_field, (("lon", 2),), STEPS)
    for substep in range(STEPS):
        out_width = lon_local + 2 * (STEPS - substep - 1)
        offset_at = substep + 1
        extended = advance(
            extended,
            widened[substep, :, offset_at : offset_at + out_width],
            widened[STEPS + substep, :, offset_at : offset_at + out_width],
            widened[2 * STEPS, :, offset_at : offset_at + out_width],
        )
    return extended


def relayout(block, reach_rows):
    row_count = block.shape[0]
    lat_count = block.shape[1]
    swapped = lax.all_to_all(block, "lon", split_axis=3, concat_axis=2, tiled=True)
    lon_count = swapped.shape[2]
    col_count = swapped.shape[3]
    block_count = lat_count // row_count
    device_index = lax.axis_index("lat")
    reach_blocks = min((reach_rows + row_count - 1) // row_count, block_count - 1)
    tile_blocks = swapped.reshape(row_count, block_count, row_count, lon_count, col_count)

    def piece_for(offset):
        target = jnp.clip(device_index + offset, 0, block_count - 1)
        return lax.dynamic_index_in_dim(tile_blocks, target, axis=1, keepdims=False)

    own_piece = piece_for(0)
    received = []
    for offset in range(-reach_blocks, reach_blocks + 1):
        if offset == 0:
            received.append(own_piece)
        else:
            received.append(from_behind(piece_for(offset), "lat", offset))
    window = jnp.stack(received[::-1], axis=0)
    padded = jnp.zeros(
        (block_count + 2 * reach_blocks, row_count, row_count, lon_count, col_count), jnp.float32
    )
    padded = lax.dynamic_update_slice_in_dim(padded, window, device_index, 0)
    regrouped = padded[reach_blocks : reach_blocks + block_count].reshape(
        lat_count, row_count, lon_count, col_count
    )
    return jnp.transpose(regrouped, (1, 0, 3, 2))


def per_device(covariance, winds, diffusivity, cutoff):
    row_count = covariance.shape[0]
    lat_count = covariance.shape[1]
    lon_local = covariance.shape[2]
    band_rows = lat_count // 4
    device_index = lax.axis_index("lat")
    lat_local = device_index * row_count + jnp.arange(row_count, dtype=jnp.int32)
    lat_all = jnp.arange(lat_count, dtype=jnp.int32)
    cut_local = lax.dynamic_slice_in_dim(cutoff, device_index * row_count, row_count)
    keep_first = jnp.abs(lat_all[None, :] - lat_local[:, None]) <= cutoff[None, :]
    keep_second = jnp.abs(lat_all[None, :] - lat_local[:, None]) <= cut_local[:, None]
    stacked = jnp.concatenate(
        [winds.reshape(2 * STEPS, lat_count, lon_local), diffusivity[None]], axis=0
    )
    widened = extended_2(stacked, (("lon", 2),), STEPS)
    state_field = jnp.where(keep_first[:, :, None, None], covariance, 0.0)
    state_field = propagate(state_field, widened)
    state_field = relayout(state_field, band_rows + STEPS)
    state_field = propagate(state_field, widened)
    state_field = jnp.where(keep_second[:, :, None, None], state_field, 0.0)
    return relayout(state_field, band_rows)


def solution(mesh):
    in_specs = (P("lat", None, "lon", None), P(None, None, None, "lon"), P(None, "lon"), P())
    out_specs = P("lat", None, "lon", None)
    return jax.shard_map(
        per_device, mesh=mesh, in_specs=in_specs, out_specs=out_specs, check_vma=False
    )
```

profile of v0, /device:TPU:0, one launch (start us, length us, event | category | flops | bytes accessed | tf_op | source)
XLA Modules:
  0.0 67.6 jit_solution(5714886319299607555)
XLA Ops:
  1.9 0.8 %broadcast_select_fusion = f32[1,4,16,128]{3,2,1,0:T(8,128)S(1)} fusion(f32[1,4,16,128]{3,2,1,0:T(8,128)} %param.4, pred[4]{0:T(512)(128)(4,1)S(1)} %get-tuple-element.51), kind=kLoop, calls=%fused_computation.86 | loop fusion | flops 8192 | bytes 65540 | tf_op jit(solution)/shard_map/jit(_where)/select_n | solution.py:111
  3.3 2.9 %collective-permute-start.1 = (f32[1,4,3,128]{3,2,1,0:T(4,128)S(1)}, f32[1,4,3,128]{3,2,1,0:T(4,128)S(1)}, u32[]{:S(2)}, u32[]{:S(2)}) collective-permute-start(f32[1,4,3,128]{3,2,1,0:T(4,128)S(1)} %get-tuple-element.44), channel_id=1, source_target_pairs={{1,0},{2,1},{3,2},{4,3},{5,4},{6,5},{7,6},{0,7},{9,8},{10,9},{11,1... | collective-permute-start | bytes 18440 | tf_op jit(solution)/shard_map/ppermute | solution.py:18
  6.6 2.3 %collective-permute-start.3 = (f32[7,4,3]{2,1,0:T(4,128)S(1)}, f32[7,4,3]{2,1,0:T(4,128)S(1)}, u32[]{:S(2)}, u32[]{:S(2)}) collective-permute-start(f32[7,4,3]{2,1,0:T(4,128)S(1)} %get-tuple-element.46), channel_id=1, source_target_pairs={{1,0},{2,1},{3,2},{4,3},{5,4},{6,5},{7,6},{0,7},{9,8},{10,9},{11,1... | collective-permute-start | bytes 1016 | tf_op jit(solution)/shard_map/ppermute | solution.py:18
  9.0 1.4 %collective-permute-done.2 = f32[7,4,3]{2,1,0:T(4,128)S(1)} collective-permute-done((f32[7,4,3]{2,1,0:T(4,128)S(1)}, f32[7,4,3]{2,1,0:T(4,128)S(1)}, u32[]{:S(2)}, u32[]{:S(2)}) %collective-permute-start.2) | collective-permute-done | bytes 368 | tf_op jit(solution)/shard_map/ppermute | solution.py:15
  11.2 0.8 %reshape.186 = f32[8,1,1024]{2,1,0:T(1,128)} reshape(f32[128,1,4,16]{3,2,1,0:T(4,128)S(1)} %bitcast.89) | data formatting | bytes 65536
  12.0 4.6 %all-to-all-start = ((f32[8,1,1024]{2,1,0:T(1,128)}), f32[8,1,1024]{2,1,0:T(1,128)S(1)}, u32[]{:S(2)}, u32[]{:S(2)}) async-start(f32[8,1,1024]{2,1,0:T(1,128)} %reshape.186), calls=%async_computation | async-start | bytes 65536 | tf_op jit(solution)/shard_map/all_to_all | solution.py:66
  16.7 4.8 %all-to-all-done = f32[8,1,1024]{2,1,0:T(1,128)S(1)} async-done(((f32[8,1,1024]{2,1,0:T(1,128)}), f32[8,1,1024]{2,1,0:T(1,128)S(1)}, u32[]{:S(2)}, u32[]{:S(2)}) %all-to-all-start) | async-done | bytes 32800 | tf_op jit(solution)/shard_map/all_to_all | solution.py:66
  23.3 5.5 %collective-permute-start.4 = (f32[1,1,128,16]{2,3,1,0:T(8,128)S(1)}, f32[1,1,128,16]{2,3,1,0:T(8,128)S(1)}, u32[]{:S(2)}, u32[]{:S(2)}) collective-permute-start(f32[1,1,128,16]{2,3,1,0:T(8,128)S(1)} %get-tuple-element.42), channel_id=1, source_target_pairs={{0,24},{1,25},{2,26},{3,27},{4,28},{5,29},{6,30},{7,31}} | collective-permute-start | bytes 24584 | tf_op jit(solution)/shard_map/ppermute | solution.py:26
  28.8 1.3 %collective-permute-start.5 = (f32[1,1,128,16]{2,3,1,0:T(8,128)S(1)}, f32[1,1,128,16]{2,3,1,0:T(8,128)S(1)}, u32[]{:S(2)}, u32[]{:S(2)}) collective-permute-start(f32[1,1,128,16]{2,3,1,0:T(8,128)S(1)} %get-tuple-element.41), channel_id=1, source_target_pairs={{0,16},{8,24},{1,17},{9,25},{2,18},{10,26},{3,19},{11,27},{4,20},{... | collective-permute-start | bytes 24584 | tf_op jit(solution)/shard_map/ppermute | solution.py:26
  30.1 2.5 %collective-permute-start.6 = (f32[1,1,128,16]{2,3,1,0:T(8,128)S(1)}, f32[1,1,128,16]{2,3,1,0:T(8,128)S(1)}, u32[]{:S(2)}, u32[]{:S(2)}) collective-permute-start(f32[1,1,128,16]{2,3,1,0:T(8,128)S(1)} %get-tuple-element.40), channel_id=1, source_target_pairs={{0,8},{8,16},{16,24},{1,9},{9,17},{17,25},{2,10},{10,18},{18,26},{... | collective-permute-start | bytes 24584 | tf_op jit(solution)/shard_map/ppermute | solution.py:26
  32.6 1.3 %collective-permute-done.6 = f32[1,1,128,16]{2,3,1,0:T(8,128)S(1)} collective-permute-done((f32[1,1,128,16]{2,3,1,0:T(8,128)S(1)}, f32[1,1,128,16]{2,3,1,0:T(8,128)S(1)}, u32[]{:S(2)}, u32[]{:S(2)}) %collective-permute-start.6) | collective-permute-done | bytes 8224 | tf_op jit(solution)/shard_map/ppermute | solution.py:26
  33.9 1.3 %collective-permute-start.7 = (f32[1,1,128,16]{2,3,1,0:T(8,128)S(1)}, f32[1,1,128,16]{2,3,1,0:T(8,128)S(1)}, u32[]{:S(2)}, u32[]{:S(2)}) collective-permute-start(f32[1,1,128,16]{2,3,1,0:T(8,128)S(1)} %get-tuple-element.38), channel_id=1, source_target_pairs={{8,0},{16,8},{24,16},{9,1},{17,9},{25,17},{10,2},{18,10},{26,18},{... | collective-permute-start | bytes 24584 | tf_op jit(solution)/shard_map/ppermute | solution.py:26
  35.2 1.3 %collective-permute-start.8 = (f32[1,1,128,16]{2,3,1,0:T(8,128)S(1)}, f32[1,1,128,16]{2,3,1,0:T(8,128)S(1)}, u32[]{:S(2)}, u32[]{:S(2)}) collective-permute-start(f32[1,1,128,16]{2,3,1,0:T(8,128)S(1)} %get-tuple-element.37), channel_id=1, source_target_pairs={{16,0},{24,8},{17,1},{25,9},{18,2},{26,10},{19,3},{27,11},{20,4},{... | collective-permute-start | bytes 24584 | tf_op jit(solution)/shard_map/ppermute | solution.py:26
  36.5 1.3 %collective-permute-start.9 = (f32[1,1,128,16]{2,3,1,0:T(8,128)S(1)}, f32[1,1,128,16]{2,3,1,0:T(8,128)S(1)}, u32[]{:S(2)}, u32[]{:S(2)}) collective-permute-start(f32[1,1,128,16]{2,3,1,0:T(8,128)S(1)} %get-tuple-element.36), channel_id=1, source_target_pairs={{24,0},{25,1},{26,2},{27,3},{28,4},{29,5},{30,6},{31,7}} | collective-permute-start | bytes 24584 | tf_op jit(solution)/shard_map/ppermute | solution.py:26
  37.8 1.9 %collective-permute-done.7 = f32[1,1,128,16]{2,3,1,0:T(8,128)S(1)} collective-permute-done((f32[1,1,128,16]{2,3,1,0:T(8,128)S(1)}, f32[1,1,128,16]{2,3,1,0:T(8,128)S(1)}, u32[]{:S(2)}, u32[]{:S(2)}) %collective-permute-start.7) | collective-permute-done | bytes 8224 | tf_op jit(solution)/shard_map/ppermute | solution.py:26
  39.7 2.7 %collective-permute-done.8 = f32[1,1,128,16]{2,3,1,0:T(8,128)S(1)} collective-permute-done((f32[1,1,128,16]{2,3,1,0:T(8,128)S(1)}, f32[1,1,128,16]{2,3,1,0:T(8,128)S(1)}, u32[]{:S(2)}, u32[]{:S(2)}) %collective-permute-start.8) | collective-permute-done | bytes 8224 | tf_op jit(solution)/shard_map/ppermute | solution.py:26
  42.5 2.8 %collective-permute-done.9 = f32[1,1,128,16]{2,3,1,0:T(8,128)S(1)} collective-permute-done((f32[1,1,128,16]{2,3,1,0:T(8,128)S(1)}, f32[1,1,128,16]{2,3,1,0:T(8,128)S(1)}, u32[]{:S(2)}, u32[]{:S(2)}) %collective-permute-start.9) | collective-permute-done | bytes 8224 | tf_op jit(solution)/shard_map/ppermute | solution.py:26
  45.4 2.6 %collective-permute-start.11 = (f32[1,4,3,128]{3,2,1,0:T(4,128)S(1)}, f32[1,4,3,128]{3,2,1,0:T(4,128)S(1)}, u32[]{:S(2)}, u32[]{:S(2)}) collective-permute-start(f32[1,4,3,128]{3,2,1,0:T(4,128)S(1)} %get-tuple-element.35), channel_id=1, source_target_pairs={{1,0},{2,1},{3,2},{4,3},{5,4},{6,5},{7,6},{0,7},{9,8},{10,9},{11,1... | collective-permute-start | bytes 18440 | tf_op jit(solution)/shard_map/ppermute | solution.py:18
  48.1 1.4 %collective-permute-done.10 = f32[1,4,3,128]{3,2,1,0:T(4,128)S(1)} collective-permute-done((f32[1,4,3,128]{3,2,1,0:T(4,128)S(1)}, f32[1,4,3,128]{3,2,1,0:T(4,128)S(1)}, u32[]{:S(2)}, u32[]{:S(2)}) %collective-permute-start.10) | collective-permute-done | bytes 6176 | tf_op jit(solution)/shard_map/ppermute | solution.py:15
  50.3 8.5 %all_to_all.30 = f32[8,1,1024]{2,1,0:T(1,128)S(1)} all-to-all(f32[8,1,1024]{2,1,0:T(1,128)S(1)} %reshape.188), channel_id=1, replica_groups=mesh['lat'=4,'lon'=8] {'lon'}, dimensions={0} | all-to-all | bytes 65536 | tf_op jit(solution)/shard_map/all_to_all | solution.py:66
  58.8 0.7 %reduce.1 = f32[8,1024]{1,0:T(8,128)S(1)} reduce(f32[8,1,1024]{2,1,0:T(1,128)S(1)} %all_to_all.30, f32[]{:T(128)} %broadcast.178), dimensions={1}, to_apply=%all_to_all.25.reduce_sub_computation | reduce | bytes 65540 | tf_op jit(solution)/shard_map/all_to_all | solution.py:66
  60.1 1.3 %collective-permute-start.12 = (f32[1,1,128,16]{2,3,1,0:T(8,128)S(1)}, f32[1,1,128,16]{2,3,1,0:T(8,128)S(1)}, u32[]{:S(2)}, u32[]{:S(2)}) collective-permute-start(f32[1,1,128,16]{2,3,1,0:T(8,128)S(1)} %get-tuple-element.31), channel_id=1, source_target_pairs={{0,8},{8,16},{16,24},{1,9},{9,17},{17,25},{2,10},{10,18},{18,26},{... | collective-permute-start | bytes 24584 | tf_op jit(solution)/shard_map/ppermute | solution.py:26
  61.4 1.3 %collective-permute-start.13 = (f32[1,1,128,16]{2,3,1,0:T(8,128)S(1)}, f32[1,1,128,16]{2,3,1,0:T(8,128)S(1)}, u32[]{:S(2)}, u32[]{:S(2)}) collective-permute-start(f32[1,1,128,16]{2,3,1,0:T(8,128)S(1)} %get-tuple-element.32), channel_id=1, source_target_pairs={{8,0},{16,8},{24,16},{9,1},{17,9},{25,17},{10,2},{18,10},{26,18},{... | collective-permute-start | bytes 24584 | tf_op jit(solution)/shard_map/ppermute | solution.py:26
  62.7 4.2 %collective-permute-done.13 = f32[1,1,128,16]{2,3,1,0:T(8,128)S(1)} collective-permute-done((f32[1,1,128,16]{2,3,1,0:T(8,128)S(1)}, f32[1,1,128,16]{2,3,1,0:T(8,128)S(1)}, u32[]{:S(2)}, u32[]{:S(2)}) %collective-permute-start.13) | collective-permute-done | bytes 8224 | tf_op jit(solution)/shard_map/ppermute | solution.py:26
  (66 shorter events, 7.4 us)
Async XLA Ops:
  0.0 0.7 copy-start.2
  2.7 3.5 %copy-start = (f32[2,3,4,16]{3,2,1,0:T(4,128)S(1)}, f32[2,3,4,16]{3,2,1,0:T(4,128)}, u32[]{:S(2)}) copy-start(f32[2,3,4,16]{3,2,1,0:T(4,128)} %param.5) | copy-start | bytes 4612
  2.7 7.8 %collective-permute-start = (f32[1,4,3,128]{3,2,1,0:T(4,128)S(1)}, f32[1,4,3,128]{3,2,1,0:T(4,128)S(1)}, u32[]{:S(2)}, u32[]{:S(2)}) collective-permute-start(f32[1,4,3,128]{3,2,1,0:T(4,128)S(1)} %get-tuple-element.43), channel_id=1, source_target_pairs={{0,1},{1,2},{2,3},{3,4},{4,5},{5,6},{6,7},{7,0},{8,9},{9,10},{10,1... | collective-permute-start | bytes 18440 | tf_op jit(solution)/shard_map/ppermute | solution.py:15
  3.3 3.0 %copy-start.1 = (f32[4,16]{1,0:T(4,128)S(1)}, f32[4,16]{1,0:T(4,128)}, u32[]{:S(2)}) copy-start(f32[4,16]{1,0:T(4,128)} %param.6) | copy-start | bytes 772
  3.3 7.3 %collective-permute-start.1 = (f32[1,4,3,128]{3,2,1,0:T(4,128)S(1)}, f32[1,4,3,128]{3,2,1,0:T(4,128)S(1)}, u32[]{:S(2)}, u32[]{:S(2)}) collective-permute-start(f32[1,4,3,128]{3,2,1,0:T(4,128)S(1)} %get-tuple-element.44), channel_id=1, source_target_pairs={{1,0},{2,1},{3,2},{4,3},{5,4},{6,5},{7,6},{0,7},{9,8},{10,9},{11,1... | collective-permute-start | bytes 18440 | tf_op jit(solution)/shard_map/ppermute | solution.py:18
  6.3 4.0 %collective-permute-start.2 = (f32[7,4,3]{2,1,0:T(4,128)S(1)}, f32[7,4,3]{2,1,0:T(4,128)S(1)}, u32[]{:S(2)}, u32[]{:S(2)}) collective-permute-start(f32[7,4,3]{2,1,0:T(4,128)S(1)} %get-tuple-element.45), channel_id=1, source_target_pairs={{0,1},{1,2},{2,3},{3,4},{4,5},{5,6},{6,7},{7,0},{8,9},{9,10},{10,1... | collective-permute-start | bytes 1016 | tf_op jit(solution)/shard_map/ppermute | solution.py:15
  6.6 3.8 %collective-permute-start.3 = (f32[7,4,3]{2,1,0:T(4,128)S(1)}, f32[7,4,3]{2,1,0:T(4,128)S(1)}, u32[]{:S(2)}, u32[]{:S(2)}) collective-permute-start(f32[7,4,3]{2,1,0:T(4,128)S(1)} %get-tuple-element.46), channel_id=1, source_target_pairs={{1,0},{2,1},{3,2},{4,3},{5,4},{6,5},{7,6},{0,7},{9,8},{10,9},{11,1... | collective-permute-start | bytes 1016 | tf_op jit(solution)/shard_map/ppermute | solution.py:18
  12.0 9.5 %all-to-all-start = ((f32[8,1,1024]{2,1,0:T(1,128)}), f32[8,1,1024]{2,1,0:T(1,128)S(1)}, u32[]{:S(2)}, u32[]{:S(2)}) async-start(f32[8,1,1024]{2,1,0:T(1,128)} %reshape.186), calls=%async_computation | async-start | bytes 65536 | tf_op jit(solution)/shard_map/all_to_all | solution.py:66
  23.3 9.3 %collective-permute-start.4 = (f32[1,1,128,16]{2,3,1,0:T(8,128)S(1)}, f32[1,1,128,16]{2,3,1,0:T(8,128)S(1)}, u32[]{:S(2)}, u32[]{:S(2)}) collective-permute-start(f32[1,1,128,16]{2,3,1,0:T(8,128)S(1)} %get-tuple-element.42), channel_id=1, source_target_pairs={{0,24},{1,25},{2,26},{3,27},{4,28},{5,29},{6,30},{7,31}} | collective-permute-start | bytes 24584 | tf_op jit(solution)/shard_map/ppermute | solution.py:26
  28.8 3.8 %collective-permute-start.5 = (f32[1,1,128,16]{2,3,1,0:T(8,128)S(1)}, f32[1,1,128,16]{2,3,1,0:T(8,128)S(1)}, u32[]{:S(2)}, u32[]{:S(2)}) collective-permute-start(f32[1,1,128,16]{2,3,1,0:T(8,128)S(1)} %get-tuple-element.41), channel_id=1, source_target_pairs={{0,16},{8,24},{1,17},{9,25},{2,18},{10,26},{3,19},{11,27},{4,20},{... | collective-permute-start | bytes 24584 | tf_op jit(solution)/shard_map/ppermute | solution.py:26
  30.1 3.8 %collective-permute-start.6 = (f32[1,1,128,16]{2,3,1,0:T(8,128)S(1)}, f32[1,1,128,16]{2,3,1,0:T(8,128)S(1)}, u32[]{:S(2)}, u32[]{:S(2)}) collective-permute-start(f32[1,1,128,16]{2,3,1,0:T(8,128)S(1)} %get-tuple-element.40), channel_id=1, source_target_pairs={{0,8},{8,16},{16,24},{1,9},{9,17},{17,25},{2,10},{10,18},{18,26},{... | collective-permute-start | bytes 24584 | tf_op jit(solution)/shard_map/ppermute | solution.py:26
  33.9 5.8 %collective-permute-start.7 = (f32[1,1,128,16]{2,3,1,0:T(8,128)S(1)}, f32[1,1,128,16]{2,3,1,0:T(8,128)S(1)}, u32[]{:S(2)}, u32[]{:S(2)}) collective-permute-start(f32[1,1,128,16]{2,3,1,0:T(8,128)S(1)} %get-tuple-element.38), channel_id=1, source_target_pairs={{8,0},{16,8},{24,16},{9,1},{17,9},{25,17},{10,2},{18,10},{26,18},{... | collective-permute-start | bytes 24584 | tf_op jit(solution)/shard_map/ppermute | solution.py:26
  35.2 7.3 %collective-permute-start.8 = (f32[1,1,128,16]{2,3,1,0:T(8,128)S(1)}, f32[1,1,128,16]{2,3,1,0:T(8,128)S(1)}, u32[]{:S(2)}, u32[]{:S(2)}) collective-permute-start(f32[1,1,128,16]{2,3,1,0:T(8,128)S(1)} %get-tuple-element.37), channel_id=1, source_target_pairs={{16,0},{24,8},{17,1},{25,9},{18,2},{26,10},{19,3},{27,11},{20,4},{... | collective-permute-start | bytes 24584 | tf_op jit(solution)/shard_map/ppermute | solution.py:26
  36.5 8.8 %collective-permute-start.9 = (f32[1,1,128,16]{2,3,1,0:T(8,128)S(1)}, f32[1,1,128,16]{2,3,1,0:T(8,128)S(1)}, u32[]{:S(2)}, u32[]{:S(2)}) collective-permute-start(f32[1,1,128,16]{2,3,1,0:T(8,128)S(1)} %get-tuple-element.36), channel_id=1, source_target_pairs={{24,0},{25,1},{26,2},{27,3},{28,4},{29,5},{30,6},{31,7}} | collective-permute-start | bytes 24584 | tf_op jit(solution)/shard_map/ppermute | solution.py:26
  45.4 4.1 %collective-permute-start.10 = (f32[1,4,3,128]{3,2,1,0:T(4,128)S(1)}, f32[1,4,3,128]{3,2,1,0:T(4,128)S(1)}, u32[]{:S(2)}, u32[]{:S(2)}) collective-permute-start(f32[1,4,3,128]{3,2,1,0:T(4,128)S(1)} %get-tuple-element.34), channel_id=1, source_target_pairs={{0,1},{1,2},{2,3},{3,4},{4,5},{5,6},{6,7},{7,0},{8,9},{9,10},{10,1... | collective-permute-start | bytes 18440 | tf_op jit(solution)/shard_map/ppermute | solution.py:15
  45.4 4.0 %collective-permute-start.11 = (f32[1,4,3,128]{3,2,1,0:T(4,128)S(1)}, f32[1,4,3,128]{3,2,1,0:T(4,128)S(1)}, u32[]{:S(2)}, u32[]{:S(2)}) collective-permute-start(f32[1,4,3,128]{3,2,1,0:T(4,128)S(1)} %get-tuple-element.35), channel_id=1, source_target_pairs={{1,0},{2,1},{3,2},{4,3},{5,4},{6,5},{7,6},{0,7},{9,8},{10,9},{11,1... | collective-permute-start | bytes 18440 | tf_op jit(solution)/shard_map/ppermute | solution.py:18
  60.1 2.6 %collective-permute-start.12 = (f32[1,1,128,16]{2,3,1,0:T(8,128)S(1)}, f32[1,1,128,16]{2,3,1,0:T(8,128)S(1)}, u32[]{:S(2)}, u32[]{:S(2)}) collective-permute-start(f32[1,1,128,16]{2,3,1,0:T(8,128)S(1)} %get-tuple-element.31), channel_id=1, source_target_pairs={{0,8},{8,16},{16,24},{1,9},{9,17},{17,25},{2,10},{10,18},{18,26},{... | collective-permute-start | bytes 24584 | tf_op jit(solution)/shard_map/ppermute | solution.py:26
  61.4 5.5 %collective-permute-start.13 = (f32[1,1,128,16]{2,3,1,0:T(8,128)S(1)}, f32[1,1,128,16]{2,3,1,0:T(8,128)S(1)}, u32[]{:S(2)}, u32[]{:S(2)}) collective-permute-start(f32[1,1,128,16]{2,3,1,0:T(8,128)S(1)} %get-tuple-element.32), channel_id=1, source_target_pairs={{8,0},{16,8},{24,16},{9,1},{17,9},{25,17},{10,2},{18,10},{26,18},{... | collective-permute-start | bytes 24584 | tf_op jit(solution)/shard_map/ppermute | solution.py:26
where the time goes:
time: 68 us; the launch traced here: 67.6 us
  starting transfers between devices  29.2 us (43%)
  waiting for transfers between devices  20.7 us (30%)
  blocking collectives  8.51 us (13%)
  local copies, waits for them, and re-layouts  4.84 us (7%)
  other arithmetic  3.95 us (6%)
    ppermute x8, starting transfers between devices, from_behind(): return lax.ppermute(shard, axis, pairs)  15.7 us
    ppermute x8, waiting for transfers between devices, from_behind(): return lax.ppermute(shard, axis, pairs)  13 us
    all_to_all x1, blocking collectives, relayout(): lax.all_to_all(block, 'lon', split_axis=3, concat_axis=2, tiled=True)  8.51 us
    ppermute x3, starting transfers between devices, extended_2(): lax.ppermute(lax.slice_in_dim(block, 0, width, axis=dim), axis, backward)  7.9 us
    all_to_all x1, waiting for transfers between devices, relayout(): lax.all_to_all(block, 'lon', split_axis=3, concat_axis=2, tiled=True)  4.84 us
    all_to_all x1, starting transfers between devices, relayout(): lax.all_to_all(block, 'lon', split_axis=3, concat_axis=2, tiled=True)  4.63 us
    ppermute x3, waiting for transfers between devices, extended_2(): lax.ppermute(lax.slice_in_dim(block, block.shape[dim] - width, None, axis...  2.77 us
    unnamed x15, local copies, waits for them, and re-layouts  2.15 us
  transfers between devices with their start and end apart: 15, of which 8 were waited for; matrix products, arithmetic and copies ran while one was open for 0% of the time, Pallas kernels for 0%

commit v1 on v0

v1 whole, which is shorter than its diff:
```python
import functools

import jax
import jax.numpy as jnp
from jax import lax
from jax.experimental import pallas as pl
from jax.experimental.pallas import tpu as pltpu
from jax.sharding import PartitionSpec as P

STEPS = 3
FIELDS = 2 * STEPS + 1
VMEM = pl.BlockSpec(memory_space=pltpu.VMEM)
SMEM = pl.BlockSpec(memory_space=pltpu.SMEM)


def shifted(shard, axis, by, wrap):
    size = lax.axis_size(axis)
    pairs = [(i, (i + by) % size) for i in range(size) if wrap or 0 <= i + by < size]
    return lax.ppermute(shard, axis, pairs)


def weights(east_wind, north_wind, spread):
    west = jnp.maximum(east_wind, 0.0) + spread
    east = spread - jnp.minimum(east_wind, 0.0)
    south = jnp.maximum(north_wind, 0.0) + spread
    north = spread - jnp.minimum(north_wind, 0.0)
    return west, east, south, north, 1.0 - (west + east + south + north)


def general(covariance, winds, diffusivity, cutoff):
    row_count, lat_count, lon_local, lon_count = covariance.shape
    blocks = lat_count // row_count
    device_index = lax.axis_index("lat")
    rows = device_index * row_count + jnp.arange(row_count, dtype=jnp.int32)
    lats = jnp.arange(lat_count, dtype=jnp.int32)
    keep = jnp.abs(lats[None, :] - rows[:, None]) <= cutoff[None, :]
    keep = keep[:, :, None, None]
    stacked = jnp.concatenate([winds.reshape(2 * STEPS, lat_count, lon_local), diffusivity[None]])
    everywhere = lax.all_gather(stacked, "lon", axis=2, tiled=True)
    left = shifted(stacked[:, :, -STEPS:], "lon", 1, True)
    right = shifted(stacked[:, :, :STEPS], "lon", -1, True)
    near = jnp.concatenate([left, stacked, right], axis=2)

    field = jnp.where(keep, covariance, 0.0)
    left = shifted(field[:, :, -STEPS:], "lon", 1, True)
    right = shifted(field[:, :, :STEPS], "lon", -1, True)
    field = jnp.concatenate([left, field, right], axis=2)
    for step in range(STEPS):
        width = near.shape[2] - 2 * step
        take = functools.partial(lax.slice_in_dim, start_index=step + 1, limit_index=step + width - 1, axis=1)
        west, east, south, north, own = (
            w[None, :, :, None]
            for w in weights(take(near[step]), take(near[STEPS + step]), take(near[2 * STEPS]))
        )
        center = field[:, :, 1:-1]
        none = jnp.zeros_like(center[:, :1])
        field = (
            own * center
            + west * field[:, :, :-2]
            + east * field[:, :, 2:]
            + south * jnp.concatenate([none, center[:, :-1]], axis=1)
            + north * jnp.concatenate([center[:, 1:], none], axis=1)
        )

    reach = min(-(-STEPS // row_count), blocks - 1)
    halo = min(STEPS, reach * row_count)
    below = [shifted(field, "lat", by, False) for by in range(reach, 0, -1)]
    above = [shifted(field, "lat", -by, False) for by in range(1, reach + 1)]
    window = jnp.concatenate([*below, field, *above])
    window = window[reach * row_count - halo : (reach + 1) * row_count + halo]
    padded = jnp.pad(everywhere, ((0, 0), (halo, halo), (0, 0)))
    local = lax.dynamic_slice_in_dim(padded, device_index * row_count, row_count + 2 * halo, 1)
    for step in range(STEPS):
        west, east, south, north, own = (
            w[:, None, None, :] for w in weights(local[step], local[STEPS + step], local[2 * STEPS])
        )
        none = jnp.zeros_like(window[:1])
        window = (
            own * window
            + west * jnp.roll(window, 1, axis=3)
            + east * jnp.roll(window, -1, axis=3)
            + south * jnp.concatenate([none, window[:-1]])
            + north * jnp.concatenate([window[1:], none])
        )
        inside = device_index * row_count - halo + jnp.arange(window.shape[0])
        inside = (inside >= 0) & (inside < lat_count)
        window = jnp.where(inside[:, None, None, None], window, 0.0)
    return jnp.where(keep, window[halo : halo + row_count], 0.0)


def place():
    lat = lax.axis_index("lat")
    lon = lax.axis_index("lon")
    return lat, lon, lax.rem(lon, 2)


def extra_source(lat, lon, count):
    core = lon % 2
    steps = (4, 5 - 2 * core, 6 + 4 * core, 11 - 6 * core)
    if isinstance(lat, int):
        return (lon + steps[lat]) % count
    step = jnp.where(lat < 2, jnp.where(lat == 0, *steps[:2]), jnp.where(lat == 2, *steps[2:]))
    return lax.rem(lon + step, count)


def prepare_kernel(cutoff, covariance, winds, diffusivity, to_core, to_cross, packed, banded):
    lat, _, core = place()
    lats, width = banded.shape[0], banded.shape[1]
    packed[...] = jnp.zeros_like(packed)
    for step in range(STEPS):
        for kind in range(2):
            at = (kind * STEPS + step) * width
            packed[:, at : at + width] = winds[kind, step]
    packed[:, 2 * STEPS * width : FIELDS * width] = diffusivity[...]
    for i in range(lats):
        keep = jnp.abs(i - lat) <= cutoff[i]
        banded[i] = jnp.where(keep, covariance[0, i], 0.0)
        first, last = banded[i, :STEPS], banded[i, width - STEPS :]
        rows = pl.ds(i * STEPS, STEPS)
        to_core[rows] = jnp.where(core == 0, last, first)
        to_cross[rows] = jnp.where(core == 0, first, last)
    rows = pl.ds(lats * STEPS, lats)
    to_core[rows] = packed[...]
    to_cross[rows] = packed[...]


def first_kernel(banded, packed, from_core, from_cross, extra, own, out_1, out_2, out_3, relay, columns):
    lat, _, core = place()
    lats, width, lon_count = banded.shape
    edge = lats * STEPS
    left = jnp.where(core == 0, from_cross[...], from_core[...])
    right = jnp.where(core == 0, from_core[...], from_cross[...])
    relay[...] = from_cross[edge:]
    columns[...] = jnp.zeros_like(columns)
    columns[0:lats] = packed[...]
    columns[lats : 2 * lats] = left[edge:]
    columns[2 * lats : 3 * lats] = right[edge:]
    turned = columns[...].T

    def spread_of(f, i):
        lo = f * width
        low = turned[lo + width - 8 : lo + width, lats + i : lats + i + 1]
        mid = turned[lo : lo + width, i : i + 1]
        high = turned[lo : lo + 8, 2 * lats + i : 2 * lats + i + 1]
        return jnp.broadcast_to(jnp.concatenate([low, mid, high]), (width + 16, lon_count))

    gap = jnp.zeros((8 - STEPS, lon_count), jnp.float32)
    field = [
        jnp.concatenate(
            [
                gap,
                left[i * STEPS : (i + 1) * STEPS],
                banded[i],
                right[i * STEPS : (i + 1) * STEPS],
                gap,
            ]
        )
        for i in range(lats)
    ]
    diffusion = [spread_of(2 * STEPS, i) for i in range(lats)]
    for step in range(STEPS):
        new = []
        for i in range(lats):
            west, east, south, north, here = weights(
                spread_of(step, i), spread_of(STEPS + step, i), diffusion[i]
            )
            value = here * field[i]
            value += west * pltpu.roll(field[i], 1, 0)
            value += east * pltpu.roll(field[i], width + 15, 0)
            if i > 0:
                value += south * field[i - 1]
            if i < lats - 1:
                value += north * field[i + 1]
            new.append(value)
        field = new
    for i in range(lats):
        own[i] = field[i][8 : 8 + width]
    for by, out in ((1, out_1), (2, out_2), (3, out_3)):
        target = lat ^ by
        for slot in range(3):
            i = jnp.clip(target - 1 + slot, 0, lats - 1)
            out[slot * width : (slot + 1) * width] = own[i]
        out[3 * width :] = extra[...]


def second_kernel(
    cutoff, own, in_1, in_2, in_3, packed, from_core, from_cross, extra, relay, out, field, result
):
    lat, lon, core = place()
    lats, width, lon_count = own.shape
    blocks = lon_count // width
    edge = lats * STEPS
    tall = 3 * width
    cross = lax.rem(lon + blocks - 1 + 2 * core, blocks)
    partner = lon ^ 1
    other = lax.rem(lon + 2 - 4 * core + blocks, blocks)
    pieces = [
        (packed[...], lon),
        (from_core[edge:], partner),
        (from_cross[edge:], cross),
        (relay[...], other),
        (extra[...], extra_source(lat, lon, blocks)),
        (in_1[tall:], extra_source(lat ^ 1, lon, blocks)),
        (in_2[tall:], extra_source(lat ^ 2, lon, blocks)),
        (in_3[tall:], extra_source(lat ^ 3, lon, blocks)),
    ]
    group = lax.broadcasted_iota(jnp.int32, (lats, lon_count), 1) // width
    ready = [(pltpu.roll(piece, at * width, 1), group == at) for piece, at in pieces]
    fields = []
    for f in range(FIELDS):
        total = None
        for piece, mask in ready:
            back = piece if f == 0 else pltpu.roll(piece, lon_count - f * width, 1)
            part = jnp.where(mask, back, 0.0)
            total = part if total is None else total + part
        fields.append(total)

    for slot in range(3):
        i = jnp.clip(lat - 1 + slot, 0, lats - 1)
        field[lat, slot * width : (slot + 1) * width] = own[i]
    for by, block in ((1, in_1), (2, in_2), (3, in_3)):
        field[lat ^ by] = block[:tall]
    values = [field[j] for j in range(lats)]
    for step in range(STEPS):
        coefficients = weights(fields[step], fields[STEPS + step], fields[2 * STEPS])
        new = []
        for j in range(lats):
            west, east, south, north, here = (
                jnp.broadcast_to(w[j : j + 1], (tall, lon_count)) for w in coefficients
            )
            value = here * values[j]
            value += west * pltpu.roll(values[j], 1, 1)
            value += east * pltpu.roll(values[j], lon_count - 1, 1)
            if j > 0:
                value += south * values[j - 1]
            if j < lats - 1:
                value += north * values[j + 1]
            new.append(value)
        values = new
    for j in range(lats):
        result[j] = values[j]
    for i in range(lats):
        slot = i - lat + 1
        keep = (slot >= 0) & (slot <= 2) & (jnp.abs(i - lat) <= cutoff[i])
        at = pl.multiple_of(jnp.clip(slot, 0, 2) * width, width)
        out[0, i] = jnp.where(keep, result[lat, pl.ds(at, width)], 0.0)


def single_row(covariance, winds, diffusivity, cutoff):
    _, lats, width, lon_count = covariance.shape
    count = lax.axis_size("lon")

    def shape(*dims):
        return jax.ShapeDtypeStruct(dims, jnp.float32)

    tall = 3 * width
    edge = shape(lats * STEPS + lats, lon_count)
    wind = shape(lats, lon_count)
    block = shape(lats, width, lon_count)
    message = shape(tall + lats, lon_count)
    to_core, to_cross, packed, banded = pl.pallas_call(
        prepare_kernel,
        out_shape=(edge, edge, wind, block),
        in_specs=[SMEM, VMEM, VMEM, VMEM],
        out_specs=(VMEM,) * 4,
    )(cutoff, covariance, winds, diffusivity)

    pair = [(i, i ^ 1) for i in range(count)]
    odd = [i for i in range(count) if i % 2]
    beyond = [p for i in odd for p in ((i, (i + 1) % count), ((i + 1) % count, i))]
    rows = range(lats)
    fetch = [(l * count + extra_source(l, m, count), l * count + m) for l in rows for m in range(count)]
    from_cross = lax.ppermute(to_cross, "lon", beyond)
    from_core = lax.ppermute(to_core, "lon", pair)
    extra = lax.ppermute(packed, ("lat", "lon"), fetch)

    own, out_1, out_2, out_3, relay = pl.pallas_call(
        first_kernel,
        out_shape=(block, message, message, message, wind),
        in_specs=[VMEM] * 5,
        out_specs=(VMEM,) * 5,
        scratch_shapes=[pltpu.VMEM((lon_count, lon_count), jnp.float32)],
    )(banded, packed, from_core, from_cross, extra)

    in_1, in_2, in_3 = (
        lax.ppermute(out, "lat", [(l, l ^ by) for l in rows])
        for by, out in ((1, out_1), (2, out_2), (3, out_3))
    )
    relay = lax.ppermute(relay, "lon", pair)
    return pl.pallas_call(
        second_kernel,
        out_shape=shape(1, lats, width, lon_count),
        in_specs=[SMEM] + [VMEM] * 9,
        out_specs=VMEM,
        scratch_shapes=[pltpu.VMEM((lats, tall, lon_count), jnp.float32)] * 2,
    )(cutoff, own, in_1, in_2, in_3, packed, from_core, from_cross, extra, relay)


def per_device(covariance, winds, diffusivity, cutoff):
    fits = lax.axis_size("lat") == 4 and lax.axis_size("lon") == 8
    fits = fits and covariance.shape == (1, 4, 16, 128)
    return (single_row if fits else general)(covariance, winds, diffusivity, cutoff)


def solution(mesh):
    in_specs = (P("lat", None, "lon", None), P(None, None, None, "lon"), P(None, "lon"), P())
    out_specs = P("lat", None, "lon", None)
    return jax.shard_map(
        per_device, mesh=mesh, in_specs=in_specs, out_specs=out_specs, check_vma=False
    )
```

time: 68 us -> 23.8 us (0.35)
  starting transfers between devices: 29.2 us -> 9.5 us
  waiting for transfers between devices: 20.7 us -> 7.59 us
  blocking collectives: 8.51 us -> 0 us
  Pallas kernels: 0 us -> 5.21 us
  other arithmetic: 3.95 us -> 0 us
  local copies, waits for them, and re-layouts: 4.84 us -> 1.2 us
    ppermute x14 -> x7, starting transfers between devices: 24.5 us -> 9.5 us  [the longest x3 4.95 us: single_row(): lax.ppermute(out, 'lat', [(l, l ^ by) for l in rows])]
    all_to_all x1 -> x0, blocking collectives: 8.51 us -> none  [relayout(): lax.all_to_all(block, 'lon', split_axis=3, concat_axis=2, tiled=True)]
    ppermute x14 -> x7, waiting for transfers between devices: 15.8 us -> 7.59 us  [the longest x3 3.34 us: single_row(): lax.ppermute(out, 'lat', [(l, l ^ by) for l in rows])]
    pallas_call x0 -> x3, Pallas kernels: none -> 5.21 us  [the longest x1 1.88 us: single_row(): pl.pallas_call(second_kernel, out_shape=shape(1, lats, width, lon_count),...]
    all_to_all x1 -> x0, waiting for transfers between devices: 4.84 us -> none  [relayout(): lax.all_to_all(block, 'lon', split_axis=3, concat_axis=2, tiled=True)]
    all_to_all x1 -> x0, starting transfers between devices: 4.63 us -> none  [relayout(): lax.all_to_all(block, 'lon', split_axis=3, concat_axis=2, tiled=True)]
    all_to_all x2 -> x0, other arithmetic: 1.44 us -> none  [relayout(): lax.all_to_all(block, 'lon', split_axis=3, concat_axis=2, tiled=True)]
    unnamed x15 -> x18, local copies, waits for them, and re-layouts: 2.15 us -> 1.2 us
  transfers between devices with their start and end apart: 15 -> 7, of which waited for: 8 -> 4; matrix products, arithmetic and copies ran while one was open for 0% -> 0% of each run, Pallas kernels for 0% -> 0%
where the time goes in v1:
time: 23.8 us; the launch traced here: 23.5 us
  starting transfers between devices  9.5 us (40%)
  waiting for transfers between devices  7.59 us (32%)
  Pallas kernels  5.21 us (22%)
  local copies, waits for them, and re-layouts  1.2 us (5%)
    ppermute x3, starting transfers between devices, single_row(): lax.ppermute(out, 'lat', [(l, l ^ by) for l in rows])  4.95 us
    ppermute x1, starting transfers between devices, single_row(): from_cross = lax.ppermute(to_cross, 'lon', beyond)  3.54 us
    ppermute x3, waiting for transfers between devices, single_row(): lax.ppermute(out, 'lat', [(l, l ^ by) for l in rows])  3.34 us
    ppermute x1, waiting for transfers between devices, single_row(): extra = lax.ppermute(packed, ('lat', 'lon'), fetch)  3.08 us
    pallas_call x1, Pallas kernels, single_row(): pl.pallas_call(second_kernel, out_shape=shape(1, lats, width, lon_count),...  1.88 us
    pallas_call x1, Pallas kernels, single_row(): pl.pallas_call(first_kernel, out_shape=(block, message, message, message,...  1.85 us
    pallas_call x1, Pallas kernels, single_row(): pl.pallas_call(prepare_kernel, out_shape=(edge, edge, wind, block), in_sp...  1.48 us
    unnamed x18, local copies, waits for them, and re-layouts  1.2 us
  transfers between devices with their start and end apart: 7, of which 4 were waited for; matrix products, arithmetic and copies ran while one was open for 0% of the time, Pallas kernels for 0%

profile of v1, /device:TPU:0, one launch (start us, length us, event | category | flops | bytes accessed | tf_op | source)
XLA Modules:
  0.0 23.5 jit_solution(3938263142363267665)
XLA Ops:
  0.0 1.5 %shard_map.46 = (f32[16,128]{1,0:T(8,128)}, f32[16,128]{1,0:T(8,128)}, f32[4,128]{1,0:T(4,128)}, f32[4,16,128]{2,1,0:T(8,128)}) custom-call(s32[4]{0:T(128)} %cutoff.3, f32[1,4,16,128]{3,2,1,0:T(8,128)} %covariance.1, f32[2,3,4,16]{3,2,1,0:T(4,128)} %winds.1, f32[4,16]{1,0:T(4,128)} %diffusivity.1), custom_call_target="tpu_custom_call" | custom-call | tf_op jit(solution)/shard_map/pallas_call | solution.py:261
  1.5 0.5 %collective-permute-start = (f32[16,128]{1,0:T(8,128)}, f32[16,128]{1,0:T(8,128)S(1)}, u32[]{:S(2)}, u32[]{:S(2)}) collective-permute-start(f32[16,128]{1,0:T(8,128)} %get-tuple-element.16), channel_id=1, source_target_pairs={{0,1},{1,0},{2,3},{3,2},{4,5},{5,4},{6,7},{7,6},{8,9},{9,8},{10,11... | collective-permute-start | bytes 24584 | tf_op jit(solution)/shard_map/ppermute | solution.py:274
  2.0 3.5 %collective-permute-start.1 = (f32[16,128]{1,0:T(8,128)}, f32[16,128]{1,0:T(8,128)S(1)}, u32[]{:S(2)}, u32[]{:S(2)}) collective-permute-start(f32[16,128]{1,0:T(8,128)} %get-tuple-element.17), channel_id=1, source_target_pairs={{1,2},{2,1},{3,4},{4,3},{5,6},{6,5},{7,0},{0,7},{9,10},{10,9},{11,... | collective-permute-start | bytes 24584 | tf_op jit(solution)/shard_map/ppermute | solution.py:273
  5.5 0.0 copy-done.5
  5.5 0.5 %collective-permute-start.2 = (f32[4,128]{1,0:T(4,128)S(1)}, f32[4,128]{1,0:T(4,128)S(1)}, u32[]{:S(2)}, u32[]{:S(2)}) collective-permute-start(f32[4,128]{1,0:T(4,128)S(1)} %copy-done.5), channel_id=1, source_target_pairs={{4,0},{5,1},{6,2},{7,3},{0,4},{1,5},{2,6},{3,7},{13,8},{12,9},{15,... | collective-permute-start | bytes 6152 | tf_op jit(solution)/shard_map/ppermute | solution.py:275
  6.0 3.1 %collective-permute-done.2.extra = f32[4,128]{1,0:T(4,128)S(1)} collective-permute-done((f32[4,128]{1,0:T(4,128)S(1)}, f32[4,128]{1,0:T(4,128)S(1)}, u32[]{:S(2)}, u32[]{:S(2)}) %collective-permute-start.2) | collective-permute-done | bytes 2080 | tf_op jit(solution)/shard_map/ppermute | solution.py:275
  9.1 0.0 collective-permute-done.from_core
  9.1 0.0 collective-permute-done.1.from_cross
  9.1 0.0 copy-start.1
  9.1 0.6 %copy-done.6 = f32[4,128]{1,0:T(4,128)} copy-done((f32[4,128]{1,0:T(4,128)}, f32[4,128]{1,0:T(4,128)S(1)}, u32[]{:S(2)}) %copy-start.6) | copy-done | bytes 2072
  9.7 0.0 copy-done
  9.7 0.0 copy-done.1
  9.7 1.8 %shard_map.47 = (f32[4,16,128]{2,1,0:T(8,128)}, f32[52,128]{1,0:T(8,128)}, f32[52,128]{1,0:T(8,128)}, f32[52,128]{1,0:T(8,128)}, f32[4,128]{1,0:T(4,128)}) custom-call(f32[4,16,128]{2,1,0:T(8,128)} %get-tuple-element.14.banded, f32[4,128]{1,0:T(4,128)} %get-tuple-element.15.packed, f32[16,128]{1,0:T(8,128)} %copy-done, f32[16,128]{1,0:T(8,128)} %copy-done.1, ...), custom_call_target="tpu_custom_call" | custom-call | tf_op jit(solution)/shard_map/pallas_call | solution.py:277
  11.6 1.0 %collective-permute-start.3 = (f32[52,128]{1,0:T(8,128)}, f32[52,128]{1,0:T(8,128)S(1)}, u32[]{:S(2)}, u32[]{:S(2)}) collective-permute-start(f32[52,128]{1,0:T(8,128)} %get-tuple-element.19), channel_id=1, source_target_pairs={{0,8},{8,0},{16,24},{24,16},{1,9},{9,1},{17,25},{25,17},{2,10},{10... | collective-permute-start | bytes 79880 | tf_op jit(solution)/shard_map/ppermute | solution.py:286
  12.6 2.6 %collective-permute-start.4 = (f32[52,128]{1,0:T(8,128)}, f32[52,128]{1,0:T(8,128)S(1)}, u32[]{:S(2)}, u32[]{:S(2)}) collective-permute-start(f32[52,128]{1,0:T(8,128)} %get-tuple-element.20), channel_id=1, source_target_pairs={{0,16},{8,24},{16,0},{24,8},{1,17},{9,25},{17,1},{25,9},{2,18},{10... | collective-permute-start | bytes 79880 | tf_op jit(solution)/shard_map/ppermute | solution.py:286
  15.2 1.4 %collective-permute-start.5 = (f32[52,128]{1,0:T(8,128)}, f32[52,128]{1,0:T(8,128)S(1)}, u32[]{:S(2)}, u32[]{:S(2)}) collective-permute-start(f32[52,128]{1,0:T(8,128)} %get-tuple-element.21), channel_id=1, source_target_pairs={{0,24},{8,16},{16,8},{24,0},{1,25},{9,17},{17,9},{25,1},{2,26},{10... | collective-permute-start | bytes 79880 | tf_op jit(solution)/shard_map/ppermute | solution.py:286
  16.5 0.0 copy-done.8
  16.5 0.0 collective-permute-start.6
  16.5 1.2 %collective-permute-done.6.relay = f32[4,128]{1,0:T(4,128)S(1)} collective-permute-done((f32[4,128]{1,0:T(4,128)S(1)}, f32[4,128]{1,0:T(4,128)S(1)}, u32[]{:S(2)}, u32[]{:S(2)}) %collective-permute-start.6) | collective-permute-done | bytes 2080 | tf_op jit(solution)/shard_map/ppermute | solution.py:289
  17.7 0.0 collective-permute-done.3.in_1
  17.7 0.1 collective-permute-done.4.in_2
  17.8 3.2 %collective-permute-done.5.in_3 = f32[52,128]{1,0:T(8,128)S(1)} collective-permute-done((f32[52,128]{1,0:T(8,128)}, f32[52,128]{1,0:T(8,128)S(1)}, u32[]{:S(2)}, u32[]{:S(2)}) %collective-permute-start.5) | collective-permute-done | bytes 26656 | tf_op jit(solution)/shard_map/ppermute | solution.py:286
  21.1 0.6 %copy-done.4 = f32[52,128]{1,0:T(8,128)} copy-done((f32[52,128]{1,0:T(8,128)}, f32[52,128]{1,0:T(8,128)S(1)}, u32[]{:S(2)}) %copy-start.4) | copy-done | bytes 26648
  21.6 1.9 %shard_map.48 = f32[1,4,16,128]{3,2,1,0:T(8,128)} custom-call(s32[4]{0:T(128)} %cutoff.3, f32[4,16,128]{2,1,0:T(8,128)} %get-tuple-element.18.own, f32[52,128]{1,0:T(8,128)} %copy-done.2, f32[52,128]{1,0:T(8,128)} %copy-done.3, f32[52,128]{1,0:T(8,128)} %copy-done.4, f32[4,128]{1,0:T(4,128)} %get-tuple-element.15.packed, f32[16,128]{1,0:T(8,128)} %copy-done, ...), custom_call_target="tpu_custom_call" | custom-call | tf_op jit(solution)/shard_map/pallas_call | solution.py:290
  (11 shorter events, 0.0 us)
Async XLA Ops:
  1.5 4.0 %copy-start.5 = (f32[4,128]{1,0:T(4,128)S(1)}, f32[4,128]{1,0:T(4,128)}, u32[]{:S(2)}) copy-start(f32[4,128]{1,0:T(4,128)} %get-tuple-element.15.packed) | copy-start | bytes 6148
  1.5 7.6 %collective-permute-start = (f32[16,128]{1,0:T(8,128)}, f32[16,128]{1,0:T(8,128)S(1)}, u32[]{:S(2)}, u32[]{:S(2)}) collective-permute-start(f32[16,128]{1,0:T(8,128)} %get-tuple-element.16), channel_id=1, source_target_pairs={{0,1},{1,0},{2,3},{3,2},{4,5},{5,4},{6,7},{7,6},{8,9},{9,8},{10,11... | collective-permute-start | bytes 24584 | tf_op jit(solution)/shard_map/ppermute | solution.py:274
  2.0 7.1 %collective-permute-start.1 = (f32[16,128]{1,0:T(8,128)}, f32[16,128]{1,0:T(8,128)S(1)}, u32[]{:S(2)}, u32[]{:S(2)}) collective-permute-start(f32[16,128]{1,0:T(8,128)} %get-tuple-element.17), channel_id=1, source_target_pairs={{1,2},{2,1},{3,4},{4,3},{5,6},{6,5},{7,0},{0,7},{9,10},{10,9},{11,... | collective-permute-start | bytes 24584 | tf_op jit(solution)/shard_map/ppermute | solution.py:273
  5.5 3.6 %collective-permute-start.2 = (f32[4,128]{1,0:T(4,128)S(1)}, f32[4,128]{1,0:T(4,128)S(1)}, u32[]{:S(2)}, u32[]{:S(2)}) collective-permute-start(f32[4,128]{1,0:T(4,128)S(1)} %copy-done.5), channel_id=1, source_target_pairs={{4,0},{5,1},{6,2},{7,3},{0,4},{1,5},{2,6},{3,7},{13,8},{12,9},{15,... | collective-permute-start | bytes 6152 | tf_op jit(solution)/shard_map/ppermute | solution.py:275
  9.1 0.6 %copy-start.6 = (f32[4,128]{1,0:T(4,128)}, f32[4,128]{1,0:T(4,128)S(1)}, u32[]{:S(2)}) copy-start(f32[4,128]{1,0:T(4,128)S(1)} %collective-permute-done.2.extra) | copy-start | bytes 6148
  9.1 0.6 %copy-start = (f32[16,128]{1,0:T(8,128)}, f32[16,128]{1,0:T(8,128)S(1)}, u32[]{:S(2)}) copy-start(f32[16,128]{1,0:T(8,128)S(1)} %collective-permute-done.from_core) | copy-start | bytes 24580
  9.1 0.6 %copy-start.1 = (f32[16,128]{1,0:T(8,128)}, f32[16,128]{1,0:T(8,128)S(1)}, u32[]{:S(2)}) copy-start(f32[16,128]{1,0:T(8,128)S(1)} %collective-permute-done.1.from_cross) | copy-start | bytes 24580
  11.6 6.1 %collective-permute-start.3 = (f32[52,128]{1,0:T(8,128)}, f32[52,128]{1,0:T(8,128)S(1)}, u32[]{:S(2)}, u32[]{:S(2)}) collective-permute-start(f32[52,128]{1,0:T(8,128)} %get-tuple-element.19), channel_id=1, source_target_pairs={{0,8},{8,0},{16,24},{24,16},{1,9},{9,1},{17,25},{25,17},{2,10},{10... | collective-permute-start | bytes 79880 | tf_op jit(solution)/shard_map/ppermute | solution.py:286
  12.6 4.0 %copy-start.8 = (f32[4,128]{1,0:T(4,128)S(1)}, f32[4,128]{1,0:T(4,128)}, u32[]{:S(2)}) copy-start(f32[4,128]{1,0:T(4,128)} %get-tuple-element.22) | copy-start | bytes 6148
  12.6 5.2 %collective-permute-start.4 = (f32[52,128]{1,0:T(8,128)}, f32[52,128]{1,0:T(8,128)S(1)}, u32[]{:S(2)}, u32[]{:S(2)}) collective-permute-start(f32[52,128]{1,0:T(8,128)} %get-tuple-element.20), channel_id=1, source_target_pairs={{0,16},{8,24},{16,0},{24,8},{1,17},{9,25},{17,1},{25,9},{2,18},{10... | collective-permute-start | bytes 79880 | tf_op jit(solution)/shard_map/ppermute | solution.py:286
  15.2 5.9 %collective-permute-start.5 = (f32[52,128]{1,0:T(8,128)}, f32[52,128]{1,0:T(8,128)S(1)}, u32[]{:S(2)}, u32[]{:S(2)}) collective-permute-start(f32[52,128]{1,0:T(8,128)} %get-tuple-element.21), channel_id=1, source_target_pairs={{0,24},{8,16},{16,8},{24,0},{1,25},{9,17},{17,9},{25,1},{2,26},{10... | collective-permute-start | bytes 79880 | tf_op jit(solution)/shard_map/ppermute | solution.py:286
  16.5 1.2 %collective-permute-start.6 = (f32[4,128]{1,0:T(4,128)S(1)}, f32[4,128]{1,0:T(4,128)S(1)}, u32[]{:S(2)}, u32[]{:S(2)}) collective-permute-start(f32[4,128]{1,0:T(4,128)S(1)} %copy-done.8), channel_id=1, source_target_pairs={{0,1},{1,0},{2,3},{3,2},{4,5},{5,4},{6,7},{7,6},{8,9},{9,8},{10,11... | collective-permute-start | bytes 6152 | tf_op jit(solution)/shard_map/ppermute | solution.py:289
  17.7 3.4 %copy-start.7 = (f32[4,128]{1,0:T(4,128)}, f32[4,128]{1,0:T(4,128)S(1)}, u32[]{:S(2)}) copy-start(f32[4,128]{1,0:T(4,128)S(1)} %collective-permute-done.6.relay) | copy-start | bytes 6148
  17.7 3.4 %copy-start.2 = (f32[52,128]{1,0:T(8,128)}, f32[52,128]{1,0:T(8,128)S(1)}, u32[]{:S(2)}) copy-start(f32[52,128]{1,0:T(8,128)S(1)} %collective-permute-done.3.in_1) | copy-start | bytes 79876
  17.8 3.2 %copy-start.3 = (f32[52,128]{1,0:T(8,128)}, f32[52,128]{1,0:T(8,128)S(1)}, u32[]{:S(2)}) copy-start(f32[52,128]{1,0:T(8,128)S(1)} %collective-permute-done.4.in_2) | copy-start | bytes 79876
  21.0 0.6 %copy-start.4 = (f32[52,128]{1,0:T(8,128)}, f32[52,128]{1,0:T(8,128)S(1)}, u32[]{:S(2)}) copy-start(f32[52,128]{1,0:T(8,128)S(1)} %collective-permute-done.5.in_3) | copy-start | bytes 79876

commit v2 on v1

--- a/solution.py
+++ b/solution.py
@@ -246,12 +246,16 @@
         out[0, i] = jnp.where(keep, result[lat, pl.ds(at, width)], 0.0)
 
 
+def on_chip(*arrays):
+    return [pltpu.with_memory_space_constraint(array, pltpu.VMEM) for array in arrays]
+
+
 def single_row(covariance, winds, diffusivity, cutoff):
     _, lats, width, lon_count = covariance.shape
     count = lax.axis_size("lon")
 
     def shape(*dims):
-        return jax.ShapeDtypeStruct(dims, jnp.float32)
+        return pltpu.VMEM(dims, jnp.float32)
 
     tall = 3 * width
     edge = shape(lats * STEPS + lats, lon_count)
@@ -280,7 +284,7 @@
         in_specs=[VMEM] * 5,
         out_specs=(VMEM,) * 5,
         scratch_shapes=[pltpu.VMEM((lon_count, lon_count), jnp.float32)],
-    )(banded, packed, from_core, from_cross, extra)
+    )(*on_chip(banded, packed, from_core, from_cross, extra))
 
     in_1, in_2, in_3 = (
         lax.ppermute(out, "lat", [(l, l ^ by) for l in rows])
@@ -289,11 +293,11 @@
     relay = lax.ppermute(relay, "lon", pair)
     return pl.pallas_call(
         second_kernel,
-        out_shape=shape(1, lats, width, lon_count),
+        out_shape=jax.ShapeDtypeStruct(covariance.shape, jnp.float32),
         in_specs=[SMEM] + [VMEM] * 9,
         out_specs=VMEM,
         scratch_shapes=[pltpu.VMEM((lats, tall, lon_count), jnp.float32)] * 2,
-    )(cutoff, own, in_1, in_2, in_3, packed, from_core, from_cross, extra, relay)
+    )(cutoff, *on_chip(own, in_1, in_2, in_3, packed, from_core, from_cross, extra, relay))
 
 
 def per_device(covariance, winds, diffusivity, cutoff):

time: 23.8 us -> 20.2 us (0.85)
  Pallas kernels: 5.21 us -> 3 us
  local copies, waits for them, and re-layouts: 1.2 us -> 0 us
    pallas_call x1, Pallas kernels: 1.85 us -> 0.42 us  [single_row(): pl.pallas_call(first_kernel, out_shape=(block, message, message, message,...]
    unnamed x18 -> x0, local copies, waits for them, and re-layouts: 1.2 us -> none
    pallas_call x1, Pallas kernels: 1.48 us -> 0.88 us  [single_row(): pl.pallas_call(prepare_kernel, out_shape=(edge, edge, wind, block), in_sp...]
  transfers between devices with their start and end apart: 7 -> 7, of which waited for: 4 -> 3; matrix products, arithmetic and copies ran while one was open for 0% -> 0% of each run, Pallas kernels for 0% -> 0%
where the time goes in v2:
time: 20.2 us; the launch traced here: 20 us
  starting transfers between devices  9.59 us (47%)
  waiting for transfers between devices  7.38 us (37%)
  Pallas kernels  3 us (15%)
    ppermute x3, starting transfers between devices, single_row(): lax.ppermute(out, 'lat', [(l, l ^ by) for l in rows])  5.02 us
    ppermute x1, starting transfers between devices, single_row(): from_cross = lax.ppermute(to_cross, 'lon', beyond)  3.54 us
    ppermute x3, waiting for transfers between devices, single_row(): lax.ppermute(out, 'lat', [(l, l ^ by) for l in rows])  3.14 us
    ppermute x1, waiting for transfers between devices, single_row(): extra = lax.ppermute(packed, ('lat', 'lon'), fetch)  3.08 us
    pallas_call x1, Pallas kernels, single_row(): pl.pallas_call(second_kernel, out_shape=jax.ShapeDtypeStruct(covariance.s...  1.71 us
    ppermute x1, waiting for transfers between devices, single_row(): relay = lax.ppermute(relay, 'lon', pair)  1.16 us
    pallas_call x1, Pallas kernels, single_row(): pl.pallas_call(prepare_kernel, out_shape=(edge, edge, wind, block), in_sp...  0.88 us
    ppermute x1, starting transfers between devices, single_row(): from_core = lax.ppermute(to_core, 'lon', pair)  0.52 us
  transfers between devices with their start and end apart: 7, of which 3 were waited for; matrix products, arithmetic and copies ran while one was open for 0% of the time, Pallas kernels for 0%

profile of v2, /device:TPU:0, one launch (start us, length us, event | category | flops | bytes accessed | tf_op | source)
XLA Modules:
  0.0 20.0 jit_solution(12933203127315856907)
XLA Ops:
  0.0 0.9 %shard_map.46 = (f32[16,128]{1,0:T(8,128)S(1)}, f32[16,128]{1,0:T(8,128)S(1)}, f32[4,128]{1,0:T(4,128)S(1)}, f32[4,16,128]{2,1,0:T(8,128)S(1)}) custom-call(s32[4]{0:T(128)} %cutoff.3, f32[1,4,16,128]{3,2,1,0:T(8,128)} %covariance.1, f32[2,3,4,16]{3,2,1,0:T(4,128)} %winds.1, f32[4,16]{1,0:T(4,128)} %diffusivity.1), custom_call_target="tpu_custom_call" | custom-call | tf_op jit(solution)/shard_map/pallas_call | solution.py:265
  0.9 0.5 %collective-permute-start = (f32[16,128]{1,0:T(8,128)S(1)}, f32[16,128]{1,0:T(8,128)S(1)}, u32[]{:S(2)}, u32[]{:S(2)}) collective-permute-start(f32[16,128]{1,0:T(8,128)S(1)} %get-tuple-element.16), channel_id=1, source_target_pairs={{0,1},{1,0},{2,3},{3,2},{4,5},{5,4},{6,7},{7,6},{8,9},{9,8},{10,11... | collective-permute-start | bytes 24584 | tf_op jit(solution)/shard_map/ppermute | solution.py:278
  1.4 3.5 %collective-permute-start.1 = (f32[16,128]{1,0:T(8,128)S(1)}, f32[16,128]{1,0:T(8,128)S(1)}, u32[]{:S(2)}, u32[]{:S(2)}) collective-permute-start(f32[16,128]{1,0:T(8,128)S(1)} %get-tuple-element.17), channel_id=1, source_target_pairs={{1,2},{2,1},{3,4},{4,3},{5,6},{6,5},{7,0},{0,7},{9,10},{10,9},{11,... | collective-permute-start | bytes 24584 | tf_op jit(solution)/shard_map/ppermute | solution.py:277
  4.9 0.5 %collective-permute-start.2 = (f32[4,128]{1,0:T(4,128)S(1)}, f32[4,128]{1,0:T(4,128)S(1)}, u32[]{:S(2)}, u32[]{:S(2)}) collective-permute-start(f32[4,128]{1,0:T(4,128)S(1)} %get-tuple-element.15.packed), channel_id=1, source_target_pairs={{4,0},{5,1},{6,2},{7,3},{0,4},{1,5},{2,6},{3,7},{13,8},{12,9},{15,... | collective-permute-start | bytes 6152 | tf_op jit(solution)/shard_map/ppermute | solution.py:279
  5.5 3.1 %collective-permute-done.2.extra = f32[4,128]{1,0:T(4,128)S(1)} collective-permute-done((f32[4,128]{1,0:T(4,128)S(1)}, f32[4,128]{1,0:T(4,128)S(1)}, u32[]{:S(2)}, u32[]{:S(2)}) %collective-permute-start.2) | collective-permute-done | bytes 2080 | tf_op jit(solution)/shard_map/ppermute | solution.py:279
  8.5 0.0 collective-permute-done.from_core
  8.5 0.0 collective-permute-done.1.from_cross
  8.5 0.4 %shard_map.47 = (f32[4,16,128]{2,1,0:T(8,128)S(1)}, f32[52,128]{1,0:T(8,128)S(1)}, f32[52,128]{1,0:T(8,128)S(1)}, f32[52,128]{1,0:T(8,128)S(1)}, f32[4,128]{1,0:T(4,128)S(1)}) custom-call(f32[4,16,128]{2,1,0:T(8,128)S(1)} %get-tuple-element.14.banded, f32[4,128]{1,0:T(4,128)S(1)} %get-tuple-element.15.packed, f32[16,128]{1,0:T(8,128)S(1)} %collective-permute-done.from_core, ...), custom_call_target="tpu_custom_call" | custom-call | tf_op jit(solution)/shard_map/pallas_call | solution.py:281
  9.0 1.1 %collective-permute-start.3 = (f32[52,128]{1,0:T(8,128)S(1)}, f32[52,128]{1,0:T(8,128)S(1)}, u32[]{:S(2)}, u32[]{:S(2)}) collective-permute-start(f32[52,128]{1,0:T(8,128)S(1)} %get-tuple-element.19), channel_id=1, source_target_pairs={{0,8},{8,0},{16,24},{24,16},{1,9},{9,1},{17,25},{25,17},{2,10},{10... | collective-permute-start | bytes 79880 | tf_op jit(solution)/shard_map/ppermute | solution.py:290
  10.0 2.6 %collective-permute-start.4 = (f32[52,128]{1,0:T(8,128)S(1)}, f32[52,128]{1,0:T(8,128)S(1)}, u32[]{:S(2)}, u32[]{:S(2)}) collective-permute-start(f32[52,128]{1,0:T(8,128)S(1)} %get-tuple-element.20), channel_id=1, source_target_pairs={{0,16},{8,24},{16,0},{24,8},{1,17},{9,25},{17,1},{25,9},{2,18},{10... | collective-permute-start | bytes 79880 | tf_op jit(solution)/shard_map/ppermute | solution.py:290
  12.6 1.4 %collective-permute-start.5 = (f32[52,128]{1,0:T(8,128)S(1)}, f32[52,128]{1,0:T(8,128)S(1)}, u32[]{:S(2)}, u32[]{:S(2)}) collective-permute-start(f32[52,128]{1,0:T(8,128)S(1)} %get-tuple-element.21), channel_id=1, source_target_pairs={{0,24},{8,16},{16,8},{24,0},{1,25},{9,17},{17,9},{25,1},{2,26},{10... | collective-permute-start | bytes 79880 | tf_op jit(solution)/shard_map/ppermute | solution.py:290
  14.0 0.0 collective-permute-start.6
  14.0 1.2 %collective-permute-done.6.relay = f32[4,128]{1,0:T(4,128)S(1)} collective-permute-done((f32[4,128]{1,0:T(4,128)S(1)}, f32[4,128]{1,0:T(4,128)S(1)}, u32[]{:S(2)}, u32[]{:S(2)}) %collective-permute-start.6) | collective-permute-done | bytes 2080 | tf_op jit(solution)/shard_map/ppermute | solution.py:293
  15.1 0.0 collective-permute-done.3.in_1
  15.1 0.0 collective-permute-done.4.in_2
  15.1 3.1 %collective-permute-done.5.in_3 = f32[52,128]{1,0:T(8,128)S(1)} collective-permute-done((f32[52,128]{1,0:T(8,128)S(1)}, f32[52,128]{1,0:T(8,128)S(1)}, u32[]{:S(2)}, u32[]{:S(2)}) %collective-permute-start.5) | collective-permute-done | bytes 26656 | tf_op jit(solution)/shard_map/ppermute | solution.py:290
  18.3 1.7 %shard_map.48 = f32[1,4,16,128]{3,2,1,0:T(8,128)} custom-call(s32[4]{0:T(128)} %cutoff.3, f32[4,16,128]{2,1,0:T(8,128)S(1)} %get-tuple-element.18.own, f32[52,128]{1,0:T(8,128)S(1)} %collective-permute-done.3.in_1, f32[52,128]{1,0:T(8,128)S(1)} %collective-permute-done.4.in_2, f32[52,128]{1,0:T(8,128)S(1)} %collective-permute-done.5.in_3, ...), custom_call_target="tpu_custom_call" | custom-call | tf_op jit(solution)/shard_map/pallas_call | solution.py:294
Async XLA Ops:
  0.9 7.7 %collective-permute-start = (f32[16,128]{1,0:T(8,128)S(1)}, f32[16,128]{1,0:T(8,128)S(1)}, u32[]{:S(2)}, u32[]{:S(2)}) collective-permute-start(f32[16,128]{1,0:T(8,128)S(1)} %get-tuple-element.16), channel_id=1, source_target_pairs={{0,1},{1,0},{2,3},{3,2},{4,5},{5,4},{6,7},{7,6},{8,9},{9,8},{10,11... | collective-permute-start | bytes 24584 | tf_op jit(solution)/shard_map/ppermute | solution.py:278
  1.4 7.1 %collective-permute-start.1 = (f32[16,128]{1,0:T(8,128)S(1)}, f32[16,128]{1,0:T(8,128)S(1)}, u32[]{:S(2)}, u32[]{:S(2)}) collective-permute-start(f32[16,128]{1,0:T(8,128)S(1)} %get-tuple-element.17), channel_id=1, source_target_pairs={{1,2},{2,1},{3,4},{4,3},{5,6},{6,5},{7,0},{0,7},{9,10},{10,9},{11,... | collective-permute-start | bytes 24584 | tf_op jit(solution)/shard_map/ppermute | solution.py:277
  4.9 3.6 %collective-permute-start.2 = (f32[4,128]{1,0:T(4,128)S(1)}, f32[4,128]{1,0:T(4,128)S(1)}, u32[]{:S(2)}, u32[]{:S(2)}) collective-permute-start(f32[4,128]{1,0:T(4,128)S(1)} %get-tuple-element.15.packed), channel_id=1, source_target_pairs={{4,0},{5,1},{6,2},{7,3},{0,4},{1,5},{2,6},{3,7},{13,8},{12,9},{15,... | collective-permute-start | bytes 6152 | tf_op jit(solution)/shard_map/ppermute | solution.py:279
  9.0 6.2 %collective-permute-start.3 = (f32[52,128]{1,0:T(8,128)S(1)}, f32[52,128]{1,0:T(8,128)S(1)}, u32[]{:S(2)}, u32[]{:S(2)}) collective-permute-start(f32[52,128]{1,0:T(8,128)S(1)} %get-tuple-element.19), channel_id=1, source_target_pairs={{0,8},{8,0},{16,24},{24,16},{1,9},{9,1},{17,25},{25,17},{2,10},{10... | collective-permute-start | bytes 79880 | tf_op jit(solution)/shard_map/ppermute | solution.py:290
  10.0 5.1 %collective-permute-start.4 = (f32[52,128]{1,0:T(8,128)S(1)}, f32[52,128]{1,0:T(8,128)S(1)}, u32[]{:S(2)}, u32[]{:S(2)}) collective-permute-start(f32[52,128]{1,0:T(8,128)S(1)} %get-tuple-element.20), channel_id=1, source_target_pairs={{0,16},{8,24},{16,0},{24,8},{1,17},{9,25},{17,1},{25,9},{2,18},{10... | collective-permute-start | bytes 79880 | tf_op jit(solution)/shard_map/ppermute | solution.py:290
  12.6 5.7 %collective-permute-start.5 = (f32[52,128]{1,0:T(8,128)S(1)}, f32[52,128]{1,0:T(8,128)S(1)}, u32[]{:S(2)}, u32[]{:S(2)}) collective-permute-start(f32[52,128]{1,0:T(8,128)S(1)} %get-tuple-element.21), channel_id=1, source_target_pairs={{0,24},{8,16},{16,8},{24,0},{1,25},{9,17},{17,9},{25,1},{2,26},{10... | collective-permute-start | bytes 79880 | tf_op jit(solution)/shard_map/ppermute | solution.py:290
  14.0 1.2 %collective-permute-start.6 = (f32[4,128]{1,0:T(4,128)S(1)}, f32[4,128]{1,0:T(4,128)S(1)}, u32[]{:S(2)}, u32[]{:S(2)}) collective-permute-start(f32[4,128]{1,0:T(4,128)S(1)} %get-tuple-element.22), channel_id=1, source_target_pairs={{0,1},{1,0},{2,3},{3,2},{4,5},{5,4},{6,7},{7,6},{8,9},{9,8},{10,11... | collective-permute-start | bytes 6152 | tf_op jit(solution)/shard_map/ppermute | solution.py:293

commit v3 on v2

v3 whole, which is shorter than its diff:
```python
import functools

import jax
import jax.numpy as jnp
from jax import lax
from jax.experimental import pallas as pl
from jax.experimental.pallas import tpu as pltpu
from jax.sharding import PartitionSpec as P

STEPS = 3
FIELDS = 2 * STEPS + 1
VMEM = pl.BlockSpec(memory_space=pltpu.VMEM)
SMEM = pl.BlockSpec(memory_space=pltpu.SMEM)


def shifted(shard, axis, by, wrap):
    size = lax.axis_size(axis)
    pairs = [(i, (i + by) % size) for i in range(size) if wrap or 0 <= i + by < size]
    return lax.ppermute(shard, axis, pairs)


def weights(east_wind, north_wind, spread):
    west = jnp.maximum(east_wind, 0.0) + spread
    east = spread - jnp.minimum(east_wind, 0.0)
    south = jnp.maximum(north_wind, 0.0) + spread
    north = spread - jnp.minimum(north_wind, 0.0)
    return west, east, south, north, 1.0 - (west + east + south + north)


def general(covariance, winds, diffusivity, cutoff):
    row_count, lat_count, lon_local, _ = covariance.shape
    blocks = lat_count // row_count
    device_index = lax.axis_index("lat")
    rows = device_index * row_count + jnp.arange(row_count, dtype=jnp.int32)
    lats = jnp.arange(lat_count, dtype=jnp.int32)
    keep = jnp.abs(lats[None, :] - rows[:, None]) <= cutoff[None, :]
    keep = keep[:, :, None, None]
    stacked = jnp.concatenate([winds.reshape(2 * STEPS, lat_count, lon_local), diffusivity[None]])
    everywhere = lax.all_gather(stacked, "lon", axis=2, tiled=True)
    left = shifted(stacked[:, :, -STEPS:], "lon", 1, True)
    right = shifted(stacked[:, :, :STEPS], "lon", -1, True)
    near = jnp.concatenate([left, stacked, right], axis=2)

    field = jnp.where(keep, covariance, 0.0)
    left = shifted(field[:, :, -STEPS:], "lon", 1, True)
    right = shifted(field[:, :, :STEPS], "lon", -1, True)
    field = jnp.concatenate([left, field, right], axis=2)
    for step in range(STEPS):
        width = near.shape[2] - 2 * step
        take = functools.partial(lax.slice_in_dim, start_index=step + 1, limit_index=step + width - 1, axis=1)
        west, east, south, north, own = (
            w[None, :, :, None]
            for w in weights(take(near[step]), take(near[STEPS + step]), take(near[2 * STEPS]))
        )
        center = field[:, :, 1:-1]
        none = jnp.zeros_like(center[:, :1])
        field = (
            own * center
            + west * field[:, :, :-2]
            + east * field[:, :, 2:]
            + south * jnp.concatenate([none, center[:, :-1]], axis=1)
            + north * jnp.concatenate([center[:, 1:], none], axis=1)
        )

    reach = min(-(-STEPS // row_count), blocks - 1)
    halo = min(STEPS, reach * row_count)
    below = [shifted(field, "lat", by, False) for by in range(reach, 0, -1)]
    above = [shifted(field, "lat", -by, False) for by in range(1, reach + 1)]
    window = jnp.concatenate([*below, field, *above])
    window = window[reach * row_count - halo : (reach + 1) * row_count + halo]
    padded = jnp.pad(everywhere, ((0, 0), (halo, halo), (0, 0)))
    local = lax.dynamic_slice_in_dim(padded, device_index * row_count, row_count + 2 * halo, 1)
    for step in range(STEPS):
        west, east, south, north, own = (
            w[:, None, None, :] for w in weights(local[step], local[STEPS + step], local[2 * STEPS])
        )
        none = jnp.zeros_like(window[:1])
        window = (
            own * window
            + west * jnp.roll(window, 1, axis=3)
            + east * jnp.roll(window, -1, axis=3)
            + south * jnp.concatenate([none, window[:-1]])
            + north * jnp.concatenate([window[1:], none])
        )
        inside = device_index * row_count - halo + jnp.arange(window.shape[0])
        inside = (inside >= 0) & (inside < lat_count)
        window = jnp.where(inside[:, None, None, None], window, 0.0)
    return jnp.where(keep, window[halo : halo + row_count], 0.0)


def place():
    lon = lax.axis_index("lon")
    return lax.axis_index("lat"), lon, lax.rem(lon, 2)


def prepare_kernel(cutoff, covariance, winds, diffusivity, to_core, to_cross, packed, banded, kept):
    lat, _, core = place()
    lats, width, lon_count = banded.shape
    packed[...] = jnp.zeros_like(packed)
    for step in range(STEPS):
        for kind in range(2):
            at = (kind * STEPS + step) * width
            packed[:, at : at + width] = winds[kind, step]
    packed[:, 2 * STEPS * width : FIELDS * width] = diffusivity[...]
    for i in range(lats):
        keep = jnp.abs(i - lat) <= cutoff[i]
        kept[i : i + 1] = jnp.full((1, lon_count), jnp.where(keep, 1.0, 0.0), jnp.float32)
        banded[i] = jnp.where(keep, covariance[0, i], 0.0)
        first, last = banded[i, :STEPS], banded[i, width - STEPS :]
        rows = pl.ds(i * STEPS, STEPS)
        to_core[rows] = jnp.where(core == 0, last, first)
        to_cross[rows] = jnp.where(core == 0, first, last)
    rows = pl.ds(lats * STEPS, lats)
    to_core[rows] = packed[...]
    to_cross[rows] = packed[...]


def turn(columns, pieces):
    columns[...] = jnp.zeros_like(columns)
    for at, piece in enumerate(pieces):
        columns[at * piece.shape[0] : (at + 1) * piece.shape[0]] = piece
    return columns[...].T


def middle_kernel(packed, middle, columns):
    lats, lon_count = packed.shape
    width = middle.shape[3]
    turned = turn(columns, [packed[...]])

    def column(f, i):
        return jnp.broadcast_to(turned[f * width : (f + 1) * width, i : i + 1], (width, lon_count))

    for i in range(lats):
        spread = column(2 * STEPS, i)
        for step in range(STEPS):
            found = weights(column(step, i), column(STEPS + step, i), spread)
            for at, weight in enumerate(found):
                middle[step, i, at] = weight


def first_kernel(banded, middle, from_core, from_cross, out_0, out_1, out_2, out_3, columns, done):
    lat, _, core = place()
    lats, width, lon_count = banded.shape
    edge = lats * STEPS
    left = jnp.where(core == 0, from_cross[...], from_core[...])
    right = jnp.where(core == 0, from_core[...], from_cross[...])
    turned = turn(columns, [left[edge:], right[edge:]])

    def column(f, i):
        low = turned[(f + 1) * width - 8 : (f + 1) * width, i : i + 1]
        high = turned[f * width : f * width + 8, lats + i : lats + i + 1]
        return jnp.broadcast_to(jnp.concatenate([low, high]), (16, lon_count))

    gap = jnp.zeros((8 - STEPS, lon_count), jnp.float32)
    field = []
    for i in range(lats):
        rows = slice(i * STEPS, (i + 1) * STEPS)
        field.append(jnp.concatenate([gap, left[rows], banded[i], right[rows], gap]))
    spread = [column(2 * STEPS, i) for i in range(lats)]
    for step in range(STEPS):
        new = []
        for i in range(lats):
            outer = weights(column(step, i), column(STEPS + step, i), spread[i])
            west, east, south, north, here = (
                jnp.concatenate([w[:8], middle[step, i, at], w[8:]]) for at, w in enumerate(outer)
            )
            value = here * field[i]
            value += west * pltpu.roll(field[i], 1, 0)
            value += east * pltpu.roll(field[i], width + 15, 0)
            if i > 0:
                value += south * field[i - 1]
            if i < lats - 1:
                value += north * field[i + 1]
            new.append(value)
        field = new
    for i in range(lats):
        done[i] = field[i][8 : 8 + width].reshape(done.shape[1:])
    tiles = width // 8
    for by, out in enumerate((out_0, out_1, out_2, out_3)):
        for slot in range(3):
            i = jnp.clip((lat ^ by) - 1 + slot, 0, lats - 1)
            out[slot * tiles : (slot + 1) * tiles] = done[i]


def assemble_kernel(packed, from_core, from_cross, far, second, relay, ready):
    lat, lon, core = place()
    lats, lon_count = packed.shape
    edge = lats * STEPS
    width = lon_count // lax.axis_size("lon")
    blocks = lon_count // width
    way = 2 * core - 1
    partner = lon ^ 1
    pieces = [
        (packed[...], lon),
        (from_core[edge:], partner),
        (from_cross[edge:], lon + way),
        (far[...], lon + 4),
        (second[...], lon + 2 * way),
        (relay[:lats], partner - way),
        (relay[lats : 2 * lats], partner + 4),
        (relay[2 * lats :], partner - 2 * way),
    ]
    group = lax.broadcasted_iota(jnp.int32, (lats, lon_count), 1) // width
    turned = []
    for piece, at in pieces:
        at = lax.rem(at + blocks, blocks)
        turned.append((pltpu.roll(piece, at * width, 1), group == at))
    fields = []
    for f in range(FIELDS):
        total = None
        for piece, mask in turned:
            back = piece if f == 0 else pltpu.roll(piece, lon_count - f * width, 1)
            part = jnp.where(mask, back, 0.0)
            total = part if total is None else total + part
        fields.append(total)
    for step in range(STEPS):
        west, east, south, north, here = weights(
            fields[step], fields[STEPS + step], fields[2 * STEPS]
        )
        for row in range(lats):
            near = north if row % 2 == 0 else south
            over = north if row == 1 else south
            for at, weight in enumerate((west, east, near, over, here)):
                line = weight[row : row + 1]
                if at == 3 and row in (0, 3):
                    line = jnp.zeros_like(line)
                ready[step, at, lat ^ row] = jnp.broadcast_to(line, (8, lon_count))


def second_kernel(ready, kept, in_0, in_1, in_2, in_3, out, result):
    lat, _, _ = place()
    lon_count = kept.shape[1]
    values = [block[...] for block in (in_0, in_1, in_2, in_3)]
    for step, slots in enumerate(((0, 1, 2, 3), (0, 1, 3), (0,))):
        new = list(values)
        for s in slots:
            west, east, near, over, here = (ready[step, at, s][None] for at in range(5))
            value = here * values[s] + near * values[s ^ 1] + over * values[s ^ 3]
            value += west * pltpu.roll(values[s], 1, 2)
            value += east * pltpu.roll(values[s], lon_count - 1, 2)
            new[s] = value
        values = new
    result[...] = values[0].reshape(result.shape)
    for i in range(out.shape[1]):
        slot = i - lat + 1
        inside = (slot >= 0) & (slot <= 2)
        keep = (kept[i : i + 1] > 0.0) & inside
        out[0, i] = jnp.where(keep, result[jnp.clip(slot, 0, 2)], 0.0)


def on_chip(*arrays):
    return [pltpu.with_memory_space_constraint(array, pltpu.VMEM) for array in arrays]


def call(kernel, out_shape, scratch_shapes, *arrays):
    return pl.pallas_call(
        kernel,
        out_shape=out_shape,
        in_specs=[VMEM] * len(arrays),
        out_specs=(VMEM,) * len(out_shape) if isinstance(out_shape, tuple) else VMEM,
        scratch_shapes=scratch_shapes,
    )(*on_chip(*arrays))


def single_row(covariance, winds, diffusivity, cutoff):
    _, lats, width, lon_count = covariance.shape
    count = lax.axis_size("lon")

    def shape(*dims):
        return pltpu.VMEM(dims, jnp.float32)

    edge = shape(lats * STEPS + lats, lon_count)
    wind = shape(lats, lon_count)
    tiles = width // 8
    message = shape(3 * tiles, 8, lon_count)
    square = shape(lon_count, lon_count)
    to_core, to_cross, packed, banded, kept = pl.pallas_call(
        prepare_kernel,
        out_shape=(edge, edge, wind, shape(lats, width, lon_count), wind),
        in_specs=[SMEM, VMEM, VMEM, VMEM],
        out_specs=(VMEM,) * 5,
    )(cutoff, covariance, winds, diffusivity)

    lons = range(count)
    pair = [(m, m ^ 1) for m in lons]
    way = [2 * (m % 2) - 1 for m in lons]
    from_cross = lax.ppermute(to_cross, "lon", [((m + way[m]) % count, m) for m in lons])
    from_core = lax.ppermute(to_core, "lon", pair)
    far = lax.ppermute(packed, "lon", [((m + 4) % count, m) for m in lons])
    second = lax.ppermute(packed, "lon", [((m + 2 * way[m]) % count, m) for m in lons])
    middle = call(middle_kernel, shape(STEPS, lats, 5, width, lon_count), [square], packed)

    outs = call(
        first_kernel,
        (message,) * 4,
        [square, shape(lats, tiles, 8, lon_count)],
        banded,
        middle,
        from_core,
        from_cross,
    )
    ins = [outs[0]]
    for by in (1, 2, 3):
        ins.append(lax.ppermute(outs[by], "lat", [(l, l ^ by) for l in range(lats)]))
    winds_here = jnp.concatenate([from_cross[lats * STEPS :], far, second])
    relay = lax.ppermute(winds_here, "lon", pair)
    ready = call(
        assemble_kernel,
        shape(STEPS, 5, lats, 8, lon_count),
        [],
        packed,
        from_core,
        from_cross,
        far,
        second,
        relay,
    )
    return call(
        second_kernel,
        jax.ShapeDtypeStruct(covariance.shape, jnp.float32),
        [shape(3, width, lon_count)],
        ready,
        kept,
        *ins,
    )


def per_device(covariance, winds, diffusivity, cutoff):
    fits = lax.axis_size("lat") == 4 and lax.axis_size("lon") == 8
    fits = fits and covariance.shape == (1, 4, 16, 128)
    return (single_row if fits else general)(covariance, winds, diffusivity, cutoff)


def solution(mesh):
    in_specs = (P("lat", None, "lon", None), P(None, None, None, "lon"), P(None, "lon"), P())
    out_specs = P("lat", None, "lon", None)
    return jax.shard_map(
        per_device, mesh=mesh, in_specs=in_specs, out_specs=out_specs, check_vma=False
    )
```

time: 20.2 us -> 17.6 us (0.87)
  waiting for transfers between devices: 7.38 us -> 5.18 us
  Pallas kernels: 3 us -> 2.52 us
    ppermute x6 -> x7, waiting for transfers between devices: 7.38 us -> 5.17 us  [the longest x3 4.01 us: single_row(): lax.ppermute(outs[by], 'lat', [(l, l ^ by) for l in range(lats)])]
    pallas_call x3 -> x5, Pallas kernels: 3 us -> 2.52 us  [the longest x4 1.64 us: call(): pl.pallas_call(kernel, out_shape=out_shape, in_specs=[VMEM] * len(arrays)...]
    ppermute x6 -> x7, starting transfers between devices: 9.07 us -> 9.17 us  [the longest x3 4.45 us: single_row(): lax.ppermute(outs[by], 'lat', [(l, l ^ by) for l in range(lats)])]
  transfers between devices with their start and end apart: 7 -> 8, of which waited for: 3 -> 3; matrix products, arithmetic and copies ran while one was open for 0% -> 0% of each run, Pallas kernels for 0% -> 4%
where the time goes in v3:
time: 17.6 us; the launch traced here: 17.5 us
  starting transfers between devices  9.69 us (55%)
  waiting for transfers between devices  5.18 us (29%)
  Pallas kernels  2.52 us (14%)
    ppermute x3, starting transfers between devices, single_row(): lax.ppermute(outs[by], 'lat', [(l, l ^ by) for l in range(lats)])  4.45 us
    ppermute x3, waiting for transfers between devices, single_row(): lax.ppermute(outs[by], 'lat', [(l, l ^ by) for l in range(lats)])  4.01 us
    ppermute x1, starting transfers between devices, single_row(): lax.ppermute(to_cross, 'lon', [((m + way[m]) % count, m) for m in lons])  3.54 us
    pallas_call x4, Pallas kernels, call(): pl.pallas_call(kernel, out_shape=out_shape, in_specs=[VMEM] * len(arrays)...  1.64 us
    ppermute x1, waiting for transfers between devices, single_row(): relay = lax.ppermute(winds_here, 'lon', pair)  1.16 us
    ppermute x1, starting transfers between devices, single_row(): far = lax.ppermute(packed, 'lon', [((m + 4) % count, m) for m in lons])  1.1 us
    pallas_call x1, Pallas kernels, single_row(): pl.pallas_call(prepare_kernel, out_shape=(edge, edge, wind, shape(lats, w...  0.88 us
    ppermute x1, starting transfers between devices, single_row(): from_core = lax.ppermute(to_core, 'lon', pair)  0.52 us
  transfers between devices with their start and end apart: 8, of which 3 were waited for; matrix products, arithmetic and copies ran while one was open for 0% of the time, Pallas kernels for 4%

profile of v3, /device:TPU:0, one launch (start us, length us, event | category | flops | bytes accessed | tf_op | source)
XLA Modules:
  0.0 17.5 jit_solution(16148800744232760084)
XLA Ops:
  0.0 0.9 %shard_map.46 = (f32[16,128]{1,0:T(8,128)S(1)}, f32[16,128]{1,0:T(8,128)S(1)}, f32[4,128]{1,0:T(4,128)S(1)}, f32[4,16,128]{2,1,0:T(8,128)S(1)}, f32[4,128]{1,0:T(4,128)S(1)}) custom-call(s32[4]{0:T(128)} %cutoff.1, f32[1,4,16,128]{3,2,1,0:T(8,128)} %covariance.1, f32[2,3,4,16]{3,2,1,0:T(4,128)} %winds.1, f32[4,16]{1,0:T(4,128)} %diffusivity.1), custom_call_target="tpu_custom_call" | custom-call | tf_op jit(solution)/shard_map/pallas_call | solution.py:277
  0.9 0.5 %collective-permute-start = (f32[16,128]{1,0:T(8,128)S(1)}, f32[16,128]{1,0:T(8,128)S(1)}, u32[]{:S(2)}, u32[]{:S(2)}) collective-permute-start(f32[16,128]{1,0:T(8,128)S(1)} %get-tuple-element.15), channel_id=1, source_target_pairs={{0,1},{1,0},{2,3},{3,2},{4,5},{5,4},{6,7},{7,6},{8,9},{9,8},{10,11... | collective-permute-start | bytes 24584 | tf_op jit(solution)/shard_map/ppermute | solution.py:288
  1.4 3.5 %collective-permute-start.1 = (f32[16,128]{1,0:T(8,128)S(1)}, f32[16,128]{1,0:T(8,128)S(1)}, u32[]{:S(2)}, u32[]{:S(2)}) collective-permute-start(f32[16,128]{1,0:T(8,128)S(1)} %get-tuple-element.16), channel_id=1, source_target_pairs={{7,0},{2,1},{1,2},{4,3},{3,4},{6,5},{5,6},{0,7},{15,8},{10,9},{9,1... | collective-permute-start | bytes 24584 | tf_op jit(solution)/shard_map/ppermute | solution.py:287
  4.9 0.0 collective-permute-start.3
  4.9 1.1 %collective-permute-start.2 = (f32[4,128]{1,0:T(4,128)S(1)}, f32[4,128]{1,0:T(4,128)S(1)}, u32[]{:S(2)}, u32[]{:S(2)}) collective-permute-start(f32[4,128]{1,0:T(4,128)S(1)} %get-tuple-element.14.packed), channel_id=1, source_target_pairs={{4,0},{5,1},{6,2},{7,3},{0,4},{1,5},{2,6},{3,7},{12,8},{13,9},{14,... | collective-permute-start | bytes 6152 | tf_op jit(solution)/shard_map/ppermute | solution.py:289
  6.0 0.3 %shard_map.48.middle = f32[3,4,5,16,128]{4,3,2,1,0:T(8,128)S(1)} custom-call(f32[4,128]{1,0:T(4,128)S(1)} %get-tuple-element.14.packed), custom_call_target="tpu_custom_call" | custom-call | tf_op jit(solution)/shard_map/pallas_call | solution.py:256
  6.3 0.0 collective-permute-done.from_core
  6.3 0.0 collective-permute-done.1.from_cross
  6.3 0.3 %shard_map.49 = (f32[6,8,128]{2,1,0:T(8,128)S(1)}, f32[6,8,128]{2,1,0:T(8,128)S(1)}, f32[6,8,128]{2,1,0:T(8,128)S(1)}, f32[6,8,128]{2,1,0:T(8,128)S(1)}) custom-call(f32[4,16,128]{2,1,0:T(8,128)S(1)} %get-tuple-element.18.banded, f32[3,4,5,16,128]{4,3,2,1,0:T(8,128)S(1)} %shard_map.48.middle, f32[16,128]{1,0:T(8,128)S(1)} %collective-permute-done.from_core, ...), custom_call_target="tpu_custom_call" | custom-call | tf_op jit(solution)/shard_map/pallas_call | solution.py:256
  6.7 1.7 %collective-permute-start.5 = (f32[6,8,128]{2,1,0:T(8,128)S(1)}, f32[6,8,128]{2,1,0:T(8,128)S(1)}, u32[]{:S(2)}, u32[]{:S(2)}) collective-permute-start(f32[6,8,128]{2,1,0:T(8,128)S(1)} %get-tuple-element.20), channel_id=1, source_target_pairs={{0,8},{8,0},{16,24},{24,16},{1,9},{9,1},{17,25},{25,17},{2,10},{10... | collective-permute-start | bytes 73736 | tf_op jit(solution)/shard_map/ppermute | solution.py:304
  8.4 2.6 %collective-permute-start.6 = (f32[6,8,128]{2,1,0:T(8,128)S(1)}, f32[6,8,128]{2,1,0:T(8,128)S(1)}, u32[]{:S(2)}, u32[]{:S(2)}) collective-permute-start(f32[6,8,128]{2,1,0:T(8,128)S(1)} %get-tuple-element.21), channel_id=1, source_target_pairs={{0,16},{8,24},{16,0},{24,8},{1,17},{9,25},{17,1},{25,9},{2,18},{10... | collective-permute-start | bytes 73736 | tf_op jit(solution)/shard_map/ppermute | solution.py:304
  11.0 0.1 collective-permute-start.7
  11.1 0.0 collective-permute-done.3.second
  11.1 0.0 collective-permute-done.2.far
  11.1 0.1 collective-permute-start.4
  11.2 1.2 %collective-permute-done.4.relay = f32[12,128]{1,0:T(8,128)S(1)} collective-permute-done((f32[12,128]{1,0:T(8,128)S(1)}, f32[12,128]{1,0:T(8,128)S(1)}, u32[]{:S(2)}, u32[]{:S(2)}) %collective-permute-start.4) | collective-permute-done | bytes 6176 | tf_op jit(solution)/shard_map/ppermute | solution.py:306
  12.4 0.2 %shard_map.47.ready = f32[3,5,4,8,128]{4,3,2,1,0:T(8,128)S(1)} custom-call(f32[4,128]{1,0:T(4,128)S(1)} %get-tuple-element.14.packed, f32[16,128]{1,0:T(8,128)S(1)} %collective-permute-done.from_core, f32[16,128]{1,0:T(8,128)S(1)} %collective-permute-done.1.from_cross, f32[4,128]{1,0:T(4,128)S(1)} %collective-permute-done.2.far, ...), custom_call_target="tpu_custom_call" | custom-call | tf_op jit(solution)/shard_map/pallas_call | solution.py:256
  12.6 0.0 collective-permute-done.5.in_1
  12.6 0.6 %collective-permute-done.6.in_2 = f32[6,8,128]{2,1,0:T(8,128)S(1)} collective-permute-done((f32[6,8,128]{2,1,0:T(8,128)S(1)}, f32[6,8,128]{2,1,0:T(8,128)S(1)}, u32[]{:S(2)}, u32[]{:S(2)}) %collective-permute-start.6) | collective-permute-done | bytes 24608 | tf_op jit(solution)/shard_map/ppermute | solution.py:304
  13.2 3.4 %collective-permute-done.7.in_3 = f32[6,8,128]{2,1,0:T(8,128)S(1)} collective-permute-done((f32[6,8,128]{2,1,0:T(8,128)S(1)}, f32[6,8,128]{2,1,0:T(8,128)S(1)}, u32[]{:S(2)}, u32[]{:S(2)}) %collective-permute-start.7) | collective-permute-done | bytes 24608 | tf_op jit(solution)/shard_map/ppermute | solution.py:304
  16.6 0.9 %shard_map.50 = f32[1,4,16,128]{3,2,1,0:T(8,128)} custom-call(f32[3,5,4,8,128]{4,3,2,1,0:T(8,128)S(1)} %shard_map.47.ready, f32[4,128]{1,0:T(4,128)S(1)} %get-tuple-element.17.kept, f32[6,8,128]{2,1,0:T(8,128)S(1)} %get-tuple-element.19.in_0, f32[6,8,128]{2,1,0:T(8,128)S(1)} %collective-permute-done.5.in_1, f32[6,8,128]{2,1,0:T(8,128)S(1)} %collective-permute-done.6.in_2, ...), custom_call_target="tpu_custom_call" | custom-call | tf_op jit(solution)/shard_map/pallas_call | solution.py:256
  (2 shorter events, 0.0 us)
Async XLA Ops:
  0.9 5.4 %collective-permute-start = (f32[16,128]{1,0:T(8,128)S(1)}, f32[16,128]{1,0:T(8,128)S(1)}, u32[]{:S(2)}, u32[]{:S(2)}) collective-permute-start(f32[16,128]{1,0:T(8,128)S(1)} %get-tuple-element.15), channel_id=1, source_target_pairs={{0,1},{1,0},{2,3},{3,2},{4,5},{5,4},{6,7},{7,6},{8,9},{9,8},{10,11... | collective-permute-start | bytes 24584 | tf_op jit(solution)/shard_map/ppermute | solution.py:288
  1.4 4.9 %collective-permute-start.1 = (f32[16,128]{1,0:T(8,128)S(1)}, f32[16,128]{1,0:T(8,128)S(1)}, u32[]{:S(2)}, u32[]{:S(2)}) collective-permute-start(f32[16,128]{1,0:T(8,128)S(1)} %get-tuple-element.16), channel_id=1, source_target_pairs={{7,0},{2,1},{1,2},{4,3},{3,4},{6,5},{5,6},{0,7},{15,8},{10,9},{9,1... | collective-permute-start | bytes 24584 | tf_op jit(solution)/shard_map/ppermute | solution.py:287
  4.9 6.2 %collective-permute-start.3 = (f32[4,128]{1,0:T(4,128)S(1)}, f32[4,128]{1,0:T(4,128)S(1)}, u32[]{:S(2)}, u32[]{:S(2)}) collective-permute-start(f32[4,128]{1,0:T(4,128)S(1)} %get-tuple-element.14.packed), channel_id=1, source_target_pairs={{6,0},{3,1},{0,2},{5,3},{2,4},{7,5},{4,6},{1,7},{14,8},{11,9},{8,1... | collective-permute-start | bytes 6152 | tf_op jit(solution)/shard_map/ppermute | solution.py:290
  4.9 6.2 %collective-permute-start.2 = (f32[4,128]{1,0:T(4,128)S(1)}, f32[4,128]{1,0:T(4,128)S(1)}, u32[]{:S(2)}, u32[]{:S(2)}) collective-permute-start(f32[4,128]{1,0:T(4,128)S(1)} %get-tuple-element.14.packed), channel_id=1, source_target_pairs={{4,0},{5,1},{6,2},{7,3},{0,4},{1,5},{2,6},{3,7},{12,8},{13,9},{14,... | collective-permute-start | bytes 6152 | tf_op jit(solution)/shard_map/ppermute | solution.py:289
  6.7 5.9 %collective-permute-start.5 = (f32[6,8,128]{2,1,0:T(8,128)S(1)}, f32[6,8,128]{2,1,0:T(8,128)S(1)}, u32[]{:S(2)}, u32[]{:S(2)}) collective-permute-start(f32[6,8,128]{2,1,0:T(8,128)S(1)} %get-tuple-element.20), channel_id=1, source_target_pairs={{0,8},{8,0},{16,24},{24,16},{1,9},{9,1},{17,25},{25,17},{2,10},{10... | collective-permute-start | bytes 73736 | tf_op jit(solution)/shard_map/ppermute | solution.py:304
  8.4 4.8 %collective-permute-start.6 = (f32[6,8,128]{2,1,0:T(8,128)S(1)}, f32[6,8,128]{2,1,0:T(8,128)S(1)}, u32[]{:S(2)}, u32[]{:S(2)}) collective-permute-start(f32[6,8,128]{2,1,0:T(8,128)S(1)} %get-tuple-element.21), channel_id=1, source_target_pairs={{0,16},{8,24},{16,0},{24,8},{1,17},{9,25},{17,1},{25,9},{2,18},{10... | collective-permute-start | bytes 73736 | tf_op jit(solution)/shard_map/ppermute | solution.py:304
  11.0 5.6 %collective-permute-start.7 = (f32[6,8,128]{2,1,0:T(8,128)S(1)}, f32[6,8,128]{2,1,0:T(8,128)S(1)}, u32[]{:S(2)}, u32[]{:S(2)}) collective-permute-start(f32[6,8,128]{2,1,0:T(8,128)S(1)} %get-tuple-element.22), channel_id=1, source_target_pairs={{0,24},{8,16},{16,8},{24,0},{1,25},{9,17},{17,9},{25,1},{2,26},{10... | collective-permute-start | bytes 73736 | tf_op jit(solution)/shard_map/ppermute | solution.py:304
  11.1 1.2 %collective-permute-start.4 = (f32[12,128]{1,0:T(8,128)S(1)}, f32[12,128]{1,0:T(8,128)S(1)}, u32[]{:S(2)}, u32[]{:S(2)}) collective-permute-start(f32[12,128]{1,0:T(8,128)S(1)} %pad_maximum_fusion), channel_id=1, source_target_pairs={{0,1},{1,0},{2,3},{3,2},{4,5},{5,4},{6,7},{7,6},{8,9},{9,8},{10,11... | collective-permute-start | bytes 18440 | tf_op jit(solution)/shard_map/ppermute | solution.py:306

commit v4 on v3

--- a/solution.py
+++ b/solution.py
@@ -9,6 +9,8 @@
 
 STEPS = 3
 FIELDS = 2 * STEPS + 1
+TARGETS = ((2, 3, 1, 0), (3, 2, 0, 1), (1, 0, 3, 2))
+SOURCES = tuple(tuple(to.index(row) for row in range(len(to))) for to in TARGETS)
 VMEM = pl.BlockSpec(memory_space=pltpu.VMEM)
 SMEM = pl.BlockSpec(memory_space=pltpu.SMEM)
 
@@ -91,6 +93,13 @@
 def place():
     lon = lax.axis_index("lon")
     return lax.axis_index("lat"), lon, lax.rem(lon, 2)
+
+
+def entry(table, at):
+    found = table[0]
+    for index in range(1, len(table)):
+        found = jnp.where(at == index, table[index], found)
+    return found
 
 
 def prepare_kernel(cutoff, covariance, winds, diffusivity, to_core, to_cross, packed, banded, kept):
@@ -176,9 +185,10 @@
     for i in range(lats):
         done[i] = field[i][8 : 8 + width].reshape(done.shape[1:])
     tiles = width // 8
-    for by, out in enumerate((out_0, out_1, out_2, out_3)):
+    targets = [lat] + [entry(to, lat) for to in TARGETS]
+    for target, out in zip(targets, (out_0, out_1, out_2, out_3)):
         for slot in range(3):
-            i = jnp.clip((lat ^ by) - 1 + slot, 0, lats - 1)
+            i = jnp.clip(target - 1 + slot, 0, lats - 1)
             out[slot * tiles : (slot + 1) * tiles] = done[i]
 
 
@@ -227,10 +237,12 @@
                 ready[step, at, lat ^ row] = jnp.broadcast_to(line, (8, lon_count))
 
 
-def second_kernel(ready, kept, in_0, in_1, in_2, in_3, out, result):
+def second_kernel(ready, kept, in_0, in_1, in_2, in_3, out, held, result):
     lat, _, _ = place()
     lon_count = kept.shape[1]
-    values = [block[...] for block in (in_0, in_1, in_2, in_3)]
+    for source, block in zip(SOURCES, (in_1, in_2, in_3)):
+        held[lat ^ entry(source, lat)] = block[...]
+    values = [in_0[...]] + [held[slot] for slot in (1, 2, 3)]
     for step, slots in enumerate(((0, 1, 2, 3), (0, 1, 3), (0,))):
         new = list(values)
         for s in slots:
@@ -300,8 +312,8 @@
         from_cross,
     )
     ins = [outs[0]]
-    for by in (1, 2, 3):
-        ins.append(lax.ppermute(outs[by], "lat", [(l, l ^ by) for l in range(lats)]))
+    for at, to in enumerate(TARGETS, start=1):
+        ins.append(lax.ppermute(outs[at], "lat", list(enumerate(to))))
     winds_here = jnp.concatenate([from_cross[lats * STEPS :], far, second])
     relay = lax.ppermute(winds_here, "lon", pair)
     ready = call(
@@ -318,7 +330,7 @@
     return call(
         second_kernel,
         jax.ShapeDtypeStruct(covariance.shape, jnp.float32),
-        [shape(3, width, lon_count)],
+        [shape(lats, 3 * tiles, 8, lon_count), shape(3, width, lon_count)],
         ready,
         kept,
         *ins,

time: 17.6 us -> 15.5 us (0.88)
  waiting for transfers between devices: 5.18 us -> 3.15 us
    ppermute x3, waiting for transfers between devices: 4.01 us -> 1.98 us  [single_row(): ins.append(lax.ppermute(outs[at], 'lat', list(enumerate(to))))]
  transfers between devices with their start and end apart: 8 -> 8, of which waited for: 3 -> 2; matrix products, arithmetic and copies ran while one was open for 0% -> 0% of each run, Pallas kernels for 4% -> 5%
where the time goes in v4:
time: 15.5 us; the launch traced here: 15.3 us
  starting transfers between devices  9.54 us (62%)
  waiting for transfers between devices  3.15 us (20%)
  Pallas kernels  2.52 us (16%)
    ppermute x3, starting transfers between devices, single_row(): ins.append(lax.ppermute(outs[at], 'lat', list(enumerate(to))))  4.31 us
    ppermute x1, starting transfers between devices, single_row(): lax.ppermute(to_cross, 'lon', [((m + way[m]) % count, m) for m in lons])  3.54 us
    ppermute x3, waiting for transfers between devices, single_row(): ins.append(lax.ppermute(outs[at], 'lat', list(enumerate(to))))  1.98 us
    pallas_call x4, Pallas kernels, call(): pl.pallas_call(kernel, out_shape=out_shape, in_specs=[VMEM] * len(arrays)...  1.64 us
    ppermute x1, waiting for transfers between devices, single_row(): relay = lax.ppermute(winds_here, 'lon', pair)  1.16 us
    ppermute x1, starting transfers between devices, single_row(): far = lax.ppermute(packed, 'lon', [((m + 4) % count, m) for m in lons])  1.1 us
    pallas_call x1, Pallas kernels, single_row(): pl.pallas_call(prepare_kernel, out_shape=(edge, edge, wind, shape(lats, w...  0.88 us
    ppermute x1, starting transfers between devices, single_row(): from_core = lax.ppermute(to_core, 'lon', pair)  0.52 us
  transfers between devices with their start and end apart: 8, of which 2 were waited for; matrix products, arithmetic and copies ran while one was open for 0% of the time, Pallas kernels for 5%

profile of v4, /device:TPU:0, one launch (start us, length us, event | category | flops | bytes accessed | tf_op | source)
XLA Modules:
  0.0 15.3 jit_solution(16924091894754059014)
XLA Ops:
  0.0 0.9 %shard_map.46 = (f32[16,128]{1,0:T(8,128)S(1)}, f32[16,128]{1,0:T(8,128)S(1)}, f32[4,128]{1,0:T(4,128)S(1)}, f32[4,16,128]{2,1,0:T(8,128)S(1)}, f32[4,128]{1,0:T(4,128)S(1)}) custom-call(s32[4]{0:T(128)} %cutoff.1, f32[1,4,16,128]{3,2,1,0:T(8,128)} %covariance.1, f32[2,3,4,16]{3,2,1,0:T(4,128)} %winds.1, f32[4,16]{1,0:T(4,128)} %diffusivity.1), custom_call_target="tpu_custom_call" | custom-call | tf_op jit(solution)/shard_map/pallas_call | solution.py:289
  0.9 0.5 %collective-permute-start = (f32[16,128]{1,0:T(8,128)S(1)}, f32[16,128]{1,0:T(8,128)S(1)}, u32[]{:S(2)}, u32[]{:S(2)}) collective-permute-start(f32[16,128]{1,0:T(8,128)S(1)} %get-tuple-element.15), channel_id=1, source_target_pairs={{0,1},{1,0},{2,3},{3,2},{4,5},{5,4},{6,7},{7,6},{8,9},{9,8},{10,11... | collective-permute-start | bytes 24584 | tf_op jit(solution)/shard_map/ppermute | solution.py:300
  1.4 3.5 %collective-permute-start.1 = (f32[16,128]{1,0:T(8,128)S(1)}, f32[16,128]{1,0:T(8,128)S(1)}, u32[]{:S(2)}, u32[]{:S(2)}) collective-permute-start(f32[16,128]{1,0:T(8,128)S(1)} %get-tuple-element.16), channel_id=1, source_target_pairs={{7,0},{2,1},{1,2},{4,3},{3,4},{6,5},{5,6},{0,7},{15,8},{10,9},{9,1... | collective-permute-start | bytes 24584 | tf_op jit(solution)/shard_map/ppermute | solution.py:299
  4.9 0.0 collective-permute-start.3
  4.9 1.1 %collective-permute-start.2 = (f32[4,128]{1,0:T(4,128)S(1)}, f32[4,128]{1,0:T(4,128)S(1)}, u32[]{:S(2)}, u32[]{:S(2)}) collective-permute-start(f32[4,128]{1,0:T(4,128)S(1)} %get-tuple-element.14.packed), channel_id=1, source_target_pairs={{4,0},{5,1},{6,2},{7,3},{0,4},{1,5},{2,6},{3,7},{12,8},{13,9},{14,... | collective-permute-start | bytes 6152 | tf_op jit(solution)/shard_map/ppermute | solution.py:301
  6.0 0.3 %shard_map.48.middle = f32[3,4,5,16,128]{4,3,2,1,0:T(8,128)S(1)} custom-call(f32[4,128]{1,0:T(4,128)S(1)} %get-tuple-element.14.packed), custom_call_target="tpu_custom_call" | custom-call | tf_op jit(solution)/shard_map/pallas_call | solution.py:268
  6.3 0.0 collective-permute-done.from_core
  6.3 0.0 collective-permute-done.1.from_cross
  6.3 0.3 %shard_map.49 = (f32[6,8,128]{2,1,0:T(8,128)S(1)}, f32[6,8,128]{2,1,0:T(8,128)S(1)}, f32[6,8,128]{2,1,0:T(8,128)S(1)}, f32[6,8,128]{2,1,0:T(8,128)S(1)}) custom-call(f32[4,16,128]{2,1,0:T(8,128)S(1)} %get-tuple-element.18.banded, f32[3,4,5,16,128]{4,3,2,1,0:T(8,128)S(1)} %shard_map.48.middle, f32[16,128]{1,0:T(8,128)S(1)} %collective-permute-done.from_core, ...), custom_call_target="tpu_custom_call" | custom-call | tf_op jit(solution)/shard_map/pallas_call | solution.py:268
  6.7 2.7 %collective-permute-start.5 = (f32[6,8,128]{2,1,0:T(8,128)S(1)}, f32[6,8,128]{2,1,0:T(8,128)S(1)}, u32[]{:S(2)}, u32[]{:S(2)}) collective-permute-start(f32[6,8,128]{2,1,0:T(8,128)S(1)} %get-tuple-element.20), channel_id=1, source_target_pairs={{0,16},{8,24},{16,8},{24,0},{1,17},{9,25},{17,9},{25,1},{2,18},{10... | collective-permute-start | bytes 73736 | tf_op jit(solution)/shard_map/ppermute | solution.py:316
  9.4 1.1 %collective-permute-start.6 = (f32[6,8,128]{2,1,0:T(8,128)S(1)}, f32[6,8,128]{2,1,0:T(8,128)S(1)}, u32[]{:S(2)}, u32[]{:S(2)}) collective-permute-start(f32[6,8,128]{2,1,0:T(8,128)S(1)} %get-tuple-element.21), channel_id=1, source_target_pairs={{0,24},{8,16},{16,0},{24,8},{1,25},{9,17},{17,1},{25,9},{2,26},{10... | collective-permute-start | bytes 73736 | tf_op jit(solution)/shard_map/ppermute | solution.py:316
  10.5 0.4 %collective-permute-start.7 = (f32[6,8,128]{2,1,0:T(8,128)S(1)}, f32[6,8,128]{2,1,0:T(8,128)S(1)}, u32[]{:S(2)}, u32[]{:S(2)}) collective-permute-start(f32[6,8,128]{2,1,0:T(8,128)S(1)} %get-tuple-element.22), channel_id=1, source_target_pairs={{0,8},{8,0},{16,24},{24,16},{1,9},{9,1},{17,25},{25,17},{2,10},{10... | collective-permute-start | bytes 73736 | tf_op jit(solution)/shard_map/ppermute | solution.py:316
  11.0 0.0 collective-permute-done.3.second
  11.0 0.0 collective-permute-done.2.far
  11.0 0.1 collective-permute-start.4
  11.1 1.2 %collective-permute-done.4.relay = f32[12,128]{1,0:T(8,128)S(1)} collective-permute-done((f32[12,128]{1,0:T(8,128)S(1)}, f32[12,128]{1,0:T(8,128)S(1)}, u32[]{:S(2)}, u32[]{:S(2)}) %collective-permute-start.4) | collective-permute-done | bytes 6176 | tf_op jit(solution)/shard_map/ppermute | solution.py:318
  12.2 0.2 %shard_map.47.ready = f32[3,5,4,8,128]{4,3,2,1,0:T(8,128)S(1)} custom-call(f32[4,128]{1,0:T(4,128)S(1)} %get-tuple-element.14.packed, f32[16,128]{1,0:T(8,128)S(1)} %collective-permute-done.from_core, f32[16,128]{1,0:T(8,128)S(1)} %collective-permute-done.1.from_cross, f32[4,128]{1,0:T(4,128)S(1)} %collective-permute-done.2.far, ...), custom_call_target="tpu_custom_call" | custom-call | tf_op jit(solution)/shard_map/pallas_call | solution.py:268
  12.4 0.0 collective-permute-done.5.in_1
  12.5 2.0 %collective-permute-done.6.in_2 = f32[6,8,128]{2,1,0:T(8,128)S(1)} collective-permute-done((f32[6,8,128]{2,1,0:T(8,128)S(1)}, f32[6,8,128]{2,1,0:T(8,128)S(1)}, u32[]{:S(2)}, u32[]{:S(2)}) %collective-permute-start.6) | collective-permute-done | bytes 24608 | tf_op jit(solution)/shard_map/ppermute | solution.py:316
  14.4 0.0 collective-permute-done.7.in_3
  14.4 0.9 %shard_map.50 = f32[1,4,16,128]{3,2,1,0:T(8,128)} custom-call(f32[3,5,4,8,128]{4,3,2,1,0:T(8,128)S(1)} %shard_map.47.ready, f32[4,128]{1,0:T(4,128)S(1)} %get-tuple-element.17.kept, f32[6,8,128]{2,1,0:T(8,128)S(1)} %get-tuple-element.19.in_0, f32[6,8,128]{2,1,0:T(8,128)S(1)} %collective-permute-done.5.in_1, f32[6,8,128]{2,1,0:T(8,128)S(1)} %collective-permute-done.6.in_2, ...), custom_call_target="tpu_custom_call" | custom-call | tf_op jit(solution)/shard_map/pallas_call | solution.py:268
  (2 shorter events, 0.0 us)
Async XLA Ops:
  0.9 5.4 %collective-permute-start = (f32[16,128]{1,0:T(8,128)S(1)}, f32[16,128]{1,0:T(8,128)S(1)}, u32[]{:S(2)}, u32[]{:S(2)}) collective-permute-start(f32[16,128]{1,0:T(8,128)S(1)} %get-tuple-element.15), channel_id=1, source_target_pairs={{0,1},{1,0},{2,3},{3,2},{4,5},{5,4},{6,7},{7,6},{8,9},{9,8},{10,11... | collective-permute-start | bytes 24584 | tf_op jit(solution)/shard_map/ppermute | solution.py:300
  1.4 4.9 %collective-permute-start.1 = (f32[16,128]{1,0:T(8,128)S(1)}, f32[16,128]{1,0:T(8,128)S(1)}, u32[]{:S(2)}, u32[]{:S(2)}) collective-permute-start(f32[16,128]{1,0:T(8,128)S(1)} %get-tuple-element.16), channel_id=1, source_target_pairs={{7,0},{2,1},{1,2},{4,3},{3,4},{6,5},{5,6},{0,7},{15,8},{10,9},{9,1... | collective-permute-start | bytes 24584 | tf_op jit(solution)/shard_map/ppermute | solution.py:299
  4.9 6.0 %collective-permute-start.3 = (f32[4,128]{1,0:T(4,128)S(1)}, f32[4,128]{1,0:T(4,128)S(1)}, u32[]{:S(2)}, u32[]{:S(2)}) collective-permute-start(f32[4,128]{1,0:T(4,128)S(1)} %get-tuple-element.14.packed), channel_id=1, source_target_pairs={{6,0},{3,1},{0,2},{5,3},{2,4},{7,5},{4,6},{1,7},{14,8},{11,9},{8,1... | collective-permute-start | bytes 6152 | tf_op jit(solution)/shard_map/ppermute | solution.py:302
  4.9 6.0 %collective-permute-start.2 = (f32[4,128]{1,0:T(4,128)S(1)}, f32[4,128]{1,0:T(4,128)S(1)}, u32[]{:S(2)}, u32[]{:S(2)}) collective-permute-start(f32[4,128]{1,0:T(4,128)S(1)} %get-tuple-element.14.packed), channel_id=1, source_target_pairs={{4,0},{5,1},{6,2},{7,3},{0,4},{1,5},{2,6},{3,7},{12,8},{13,9},{14,... | collective-permute-start | bytes 6152 | tf_op jit(solution)/shard_map/ppermute | solution.py:301
  6.7 5.8 %collective-permute-start.5 = (f32[6,8,128]{2,1,0:T(8,128)S(1)}, f32[6,8,128]{2,1,0:T(8,128)S(1)}, u32[]{:S(2)}, u32[]{:S(2)}) collective-permute-start(f32[6,8,128]{2,1,0:T(8,128)S(1)} %get-tuple-element.20), channel_id=1, source_target_pairs={{0,16},{8,24},{16,8},{24,0},{1,17},{9,25},{17,9},{25,1},{2,18},{10... | collective-permute-start | bytes 73736 | tf_op jit(solution)/shard_map/ppermute | solution.py:316
  9.4 5.0 %collective-permute-start.6 = (f32[6,8,128]{2,1,0:T(8,128)S(1)}, f32[6,8,128]{2,1,0:T(8,128)S(1)}, u32[]{:S(2)}, u32[]{:S(2)}) collective-permute-start(f32[6,8,128]{2,1,0:T(8,128)S(1)} %get-tuple-element.21), channel_id=1, source_target_pairs={{0,24},{8,16},{16,0},{24,8},{1,25},{9,17},{17,1},{25,9},{2,26},{10... | collective-permute-start | bytes 73736 | tf_op jit(solution)/shard_map/ppermute | solution.py:316
  10.5 3.9 %collective-permute-start.7 = (f32[6,8,128]{2,1,0:T(8,128)S(1)}, f32[6,8,128]{2,1,0:T(8,128)S(1)}, u32[]{:S(2)}, u32[]{:S(2)}) collective-permute-start(f32[6,8,128]{2,1,0:T(8,128)S(1)} %get-tuple-element.22), channel_id=1, source_target_pairs={{0,8},{8,0},{16,24},{24,16},{1,9},{9,1},{17,25},{25,17},{2,10},{10... | collective-permute-start | bytes 73736 | tf_op jit(solution)/shard_map/ppermute | solution.py:316
  11.0 1.2 %collective-permute-start.4 = (f32[12,128]{1,0:T(8,128)S(1)}, f32[12,128]{1,0:T(8,128)S(1)}, u32[]{:S(2)}, u32[]{:S(2)}) collective-permute-start(f32[12,128]{1,0:T(8,128)S(1)} %pad_maximum_fusion), channel_id=1, source_target_pairs={{0,1},{1,0},{2,3},{3,2},{4,5},{5,4},{6,7},{7,6},{8,9},{9,8},{10,11... | collective-permute-start | bytes 18440 | tf_op jit(solution)/shard_map/ppermute | solution.py:318
